TPU v7x, 256 devices: a whole 4x4x8 slice. The times are simulated.
256 devices in a mesh: seq: 16 (over x, y_hi, core), fsdp: 16 (over z, y_lo).
Axes of the slice: x: 4, y: 4 (y_hi: 2, y_lo: 2; y = y_hi * 2 + y_lo), z: 8, core: 2. Of those that a mesh axis runs over, the one named last changes fastest.
Arguments:
- hidden: bfloat16 [32768, 8192], P(('seq', 'fsdp')), may hold values from -24 to 24
- kv_blocks: bfloat16 [8192, 1024], P('fsdp'), may hold values from -0.0625 to 0.0625
- kv_scale: float32 [64, 8], P('fsdp'), may hold values from 0.5 to 2
- queries: bfloat16 [32768, 4096], P(('seq', 'fsdp')), may hold values from -24 to 24
- grad_out: bfloat16 [32768, 4096], P(('seq', 'fsdp')), may hold values from -6 to 6
Outputs:
- attn_out: bfloat16 [32768, 4096], P(('seq', 'fsdp'))
- grad_queries: bfloat16 [32768, 4096], P(('seq', 'fsdp'))
- grad_hidden: bfloat16 [32768, 8192], P(('seq', 'fsdp'))
- weight_grad: float32 [8192, 1024], P('fsdp')
All inputs are finite; a program needn't handle non-finite values.
Results may differ from a plain program's by a relative error of at most 0.0075.
The roundings to bfloat16 on the way count: a program that leaves them out, or rounds other values in their place, can miss the bound.
Values may be sent and summed in bfloat16 or wider, within the bound.
No kernel may reach another device: no remote copies, remote signals or barrier semaphores. Data moves between devices by JAX's collectives and lax.ppermute only.
A program may use at most 128 MiB of HBM per device.

v0:
```python
import jax
import jax.numpy as jnp
from jax import lax
from jax.sharding import Mesh
from jax.sharding import PartitionSpec as P

HEADS = 32
KV_HEADS = 4
HEAD = 128
QB = 128
FSDP = ("fsdp_0", "fsdp_1")
SEQ_FSDP = ("seq", "fsdp_0", "fsdp_1")


NEG = -1e30


def gather_axes(value, axes, dim):
    if not axes:
        return value
    nearer = lax.all_gather(value, axes[-1], axis=dim, tiled=True)
    return gather_axes(nearer, axes[:-1], dim)


def shifted(block, axis, distance):
    devices = range(lax.axis_size(axis))
    route = [(i - distance, i) for i in devices if i - distance in devices]
    return lax.ppermute(block, axis, route)


def dequantize(blocks, scale):
    rows, cols = blocks.shape
    grid = blocks.astype(jnp.float32).reshape(scale.shape[0], QB, scale.shape[1], QB)
    return (grid * scale[:, None, :, None]).reshape(rows, cols).astype(jnp.bfloat16)


def attend_group(operands, allowed):
    qgrp, kgrp, vgrp, ggrp = operands
    factor = 1.0 / float(HEAD) ** 0.5
    scores = jnp.einsum("rhd,kd->rhk", qgrp, kgrp, preferred_element_type=jnp.float32) * factor
    scores = jnp.where(allowed[:, None, :], scores, NEG)
    top = jnp.max(scores, axis=-1, keepdims=True)
    expd = jnp.exp(scores - top)
    probs = expd / jnp.sum(expd, axis=-1, keepdims=True)
    probs_b = probs.astype(jnp.bfloat16)
    output = jnp.einsum("rhk,kd->rhd", probs_b, vgrp, preferred_element_type=jnp.float32).astype(
        jnp.bfloat16
    )
    dprobs = jnp.einsum("rhd,kd->rhk", ggrp, vgrp, preferred_element_type=jnp.float32)
    delta = jnp.sum(probs * dprobs, axis=-1, keepdims=True)
    dscores = (probs * (dprobs - delta) * factor).astype(jnp.bfloat16)
    gradq = jnp.einsum("rhk,kd->rhd", dscores, kgrp, preferred_element_type=jnp.float32).astype(
        jnp.bfloat16
    )
    gradk = jnp.einsum("rhk,rhd->kd", dscores, qgrp, preferred_element_type=jnp.float32)
    gradv = jnp.einsum("rhk,rhd->kd", probs_b, ggrp, preferred_element_type=jnp.float32)
    return (output, gradq, gradk, gradv)


def attend(queries, window, grad_out, allowed):
    rows = queries.shape[0]
    count = window.shape[0]
    group = HEADS // KV_HEADS
    kvw = KV_HEADS * HEAD
    qgrp = queries.reshape(rows, KV_HEADS, group, HEAD).transpose(1, 0, 2, 3)
    ggrp = grad_out.reshape(rows, KV_HEADS, group, HEAD).transpose(1, 0, 2, 3)
    kgrp = window[:, :kvw].reshape(count, KV_HEADS, HEAD).transpose(1, 0, 2)
    vgrp = window[:, kvw:].reshape(count, KV_HEADS, HEAD).transpose(1, 0, 2)
    output, gradq, gradk, gradv = lax.map(
        lambda ops: attend_group(ops, allowed), (qgrp, kgrp, vgrp, ggrp)
    )
    output = output.transpose(1, 0, 2, 3).reshape(rows, HEADS * HEAD)
    gradq = gradq.transpose(1, 0, 2, 3).reshape(rows, HEADS * HEAD)
    gradk = gradk.transpose(1, 0, 2).reshape(count, kvw)
    gradv = gradv.transpose(1, 0, 2).reshape(count, kvw)
    return (output, gradq, jnp.concatenate([gradk, gradv], axis=1))


def body(hidden, kv_blocks, kv_scale, queries, grad_out):
    tok = hidden.shape[0]
    groups = lax.axis_size(FSDP)
    reach = groups // 2
    place = lax.axis_index(FSDP)
    linear = lax.axis_index("seq") * groups + place
    weights = dequantize(kv_blocks, kv_scale)
    columns = lax.all_to_all(hidden, FSDP, split_axis=1, concat_axis=0, tiled=True)
    whole = gather_axes(weights, FSDP, 0)
    kv = jnp.dot(hidden, whole, preferred_element_type=jnp.float32).astype(jnp.bfloat16)
    pieces = []
    for offset in range(reach, 0, -1):
        pieces.append(shifted(kv, SEQ_FSDP, offset))
    window = jnp.concatenate(pieces + [kv], axis=0)
    base = linear * tok
    qpos = base + jnp.arange(tok, dtype=jnp.int32)
    kpos = base - reach * tok + jnp.arange((reach + 1) * tok, dtype=jnp.int32)
    span = reach * tok
    allowed = (
        (qpos[:, None] - kpos[None, :] < span)
        & (kpos[None, :] <= qpos[:, None])
        & (kpos[None, :] >= 0)
    )
    attn_out, grad_queries, dwin = attend(queries, window, grad_out, allowed)
    total = dwin[reach * tok :]
    inside = total
    for offset in range(1, reach + 1):
        piece = dwin[(reach - offset) * tok : (reach - offset + 1) * tok]
        returned = shifted(piece, SEQ_FSDP, -offset)
        total = total + returned
        inside = inside + jnp.where(place + offset < groups, returned, jnp.zeros_like(returned))
    all_grad = total.astype(jnp.bfloat16)
    seg_grad = inside.astype(jnp.bfloat16)
    grad_hidden = lax.dot_general(
        seg_grad, whole, (((1,), (1,)), ((), ())), preferred_element_type=jnp.float32
    ).astype(jnp.bfloat16)
    shard_grad = lax.dot_general(
        columns,
        lax.all_gather(all_grad, FSDP, axis=0, tiled=True),
        (((0,), (0,)), ((), ())),
        preferred_element_type=jnp.float32,
    )
    weight_grad = lax.psum(shard_grad, "seq")
    return (attn_out, grad_queries, grad_hidden, weight_grad)


def solution(mesh):
    finer = Mesh(mesh.devices.reshape(mesh.shape["seq"], 8, 2), ("seq", "fsdp_0", "fsdp_1"))
    placed = (P(SEQ_FSDP, None), P(FSDP, None), P(FSDP, None), P(SEQ_FSDP, None), P(SEQ_FSDP, None))
    return jax.shard_map(
        body,
        mesh=finer,
        in_specs=placed,
        out_specs=(P(SEQ_FSDP, None), P(SEQ_FSDP, None), P(SEQ_FSDP, None), P(FSDP, None)),
        check_vma=False,
    )
```

profile of v0, /device:TPU:1, one launch (start us, length us, event | category | flops | bytes accessed | tf_op | source)
XLA Modules:
  0.0 1012.2 jit_solution(2476808071577137936)
XLA Ops:
  10.0 42.4 %all-gather.4.cloned.1.call-done = bf16[1024,1024]{1,0:T(8,128)(2,1)} async-done(((bf16[512,1024]{1,0:T(8,128)(2,1)}), bf16[1024,1024]{1,0:T(8,128)(2,1)}) %all-gather.4.cloned.1.call-update) | async-done | bytes 2097168 | tf_op jit(solution)/shard_map/all_gather | solution.py:21
  52.5 175.5 %all-gather.6.cloned.1.call-done = bf16[8192,1024]{1,0:T(8,128)(2,1)} async-done(((bf16[1024,1024]{1,0:T(8,128)(2,1)}), bf16[8192,1024]{1,0:T(8,128)(2,1)}) %all-gather.6.cloned.1.call-update) | async-done | bytes 16777232 | tf_op jit(solution)/shard_map/all_gather | solution.py:21
  228.0 8.1 fusion.100
  245.0 5.8 collective-permute-start.2
  271.7 18.8 %collective-permute-done.2 = bf16[128,1024]{1,0:T(8,128)(2,1)S(1)} collective-permute-done((bf16[128,1024]{1,0:T(8,128)(2,1)S(1)}, bf16[128,1024]{1,0:T(8,128)(2,1)S(1)}, u32[]{:S(2)}, u32[]{:S(2)}) %collective-permute-start.2) | collective-permute-done | bytes 262176 | tf_op jit(solution)/shard_map/ppermute | solution.py:28
  292.5 13.1 %collective-permute-done.3 = bf16[128,1024]{1,0:T(8,128)(2,1)S(1)} collective-permute-done((bf16[128,1024]{1,0:T(8,128)(2,1)S(1)}, bf16[128,1024]{1,0:T(8,128)(2,1)S(1)}, u32[]{:S(2)}, u32[]{:S(2)}) %collective-permute-start.3) | collective-permute-done | bytes 262176 | tf_op jit(solution)/shard_map/ppermute | solution.py:28
  305.6 7.8 collective-permute-done.5
  313.4 8.5 collective-permute-done.6
  321.9 12.2 %collective-permute-done.7 = bf16[128,1024]{1,0:T(8,128)(2,1)S(1)} collective-permute-done((bf16[128,1024]{1,0:T(8,128)(2,1)S(1)}, bf16[128,1024]{1,0:T(8,128)(2,1)S(1)}, u32[]{:S(2)}, u32[]{:S(2)}) %collective-permute-start.7) | collective-permute-done | bytes 262176 | tf_op jit(solution)/shard_map/ppermute | solution.py:28
  336.1 180.6 %while.17 = (s32[]{:T(128)}, bf16[4,128,8,128]{3,1,2,0:T(8,128)(2,1)}, bf16[4,128,8,128]{3,1,2,0:T(8,128)(2,1)}, f32[4,1152,128]{1,2,0:T(8,128)S(1)}, f32[4,1152...) while((s32[]{:T(128)}, ...), condition=%wide.region_4.5_spmd.clone, body=%wide.region_0.4_spmd.clone.sunk | while | flops 2449958400 | bytes 52865276 | solution.py:69
  346.7 12.1 %fusion.171 = f32[4,1152,128]{1,2,0:T(8,128)S(1)} fusion(f32[4,1152,128]{1,2,0:T(8,128)S(1)} %get-tuple-element.259, s32[]{:T(128)} %get-tuple-element.256, f32[128,8,1152]{2,0,1:T(8,128)} %fusion.169, bf16[4,128,8,128]{1,3,2,0:T(8,128)(2,1)} %get-tuple-element.274, f32[128,8,1152]{2,0,1:T(8,128)} %get-tuple-element.242, ...), kind=kOutput, calls=%fused_computation.17.clone.1 | convolution fusion | flops 310249600 | bytes 19735552 | tf_op jit(solution)/shard_map/while/body/eval_jaxpr/rhk,rhd->kd/dot_general | solution.py:55
  358.7 12.5 %fusion.170 = bf16[4,128,8,128]{3,1,2,0:T(8,128)(2,1)} fusion(bf16[4,128,8,128]{3,1,2,0:T(8,128)(2,1)} %get-tuple-element.258, s32[]{:T(128)} %get-tuple-element.256, f32[128,8,1152]{2,0,1:T(8,128)} %fusion.169, bf16[4,1152,128]{2,1,0:T(8,128)(2,1)} %get-tuple-element.275, f32[128,8,1152]{2,0,1:T(8,128)} %get-tuple-element.242, ...), kind=kOutput, calls=%fused_computation.28.clone.1 | convolution fusion | flops 310380672 | bytes 19440640 | tf_op jit(solution)/shard_map/while/body/eval_jaxpr/rhk,kd->rhd/dot_general | solution.py:52
  382.1 5.7 exponential_reduce_fusion.2
  391.8 12.1 %fusion.171 = f32[4,1152,128]{1,2,0:T(8,128)S(1)} fusion(f32[4,1152,128]{1,2,0:T(8,128)S(1)} %get-tuple-element.259, s32[]{:T(128)} %get-tuple-element.256, f32[128,8,1152]{2,0,1:T(8,128)} %fusion.169, bf16[4,128,8,128]{1,3,2,0:T(8,128)(2,1)} %get-tuple-element.274, f32[128,8,1152]{2,0,1:T(8,128)} %get-tuple-element.242, ...), kind=kOutput, calls=%fused_computation.17.clone.1 | convolution fusion | flops 310249600 | bytes 19735552 | tf_op jit(solution)/shard_map/while/body/eval_jaxpr/rhk,rhd->kd/dot_general | solution.py:55
  403.9 12.5 %fusion.170 = bf16[4,128,8,128]{3,1,2,0:T(8,128)(2,1)} fusion(bf16[4,128,8,128]{3,1,2,0:T(8,128)(2,1)} %get-tuple-element.258, s32[]{:T(128)} %get-tuple-element.256, f32[128,8,1152]{2,0,1:T(8,128)} %fusion.169, bf16[4,1152,128]{2,1,0:T(8,128)(2,1)} %get-tuple-element.275, f32[128,8,1152]{2,0,1:T(8,128)} %get-tuple-element.242, ...), kind=kOutput, calls=%fused_computation.28.clone.1 | convolution fusion | flops 310380672 | bytes 19440640 | tf_op jit(solution)/shard_map/while/body/eval_jaxpr/rhk,kd->rhd/dot_general | solution.py:52
  437.0 12.1 %fusion.171 = f32[4,1152,128]{1,2,0:T(8,128)S(1)} fusion(f32[4,1152,128]{1,2,0:T(8,128)S(1)} %get-tuple-element.259, s32[]{:T(128)} %get-tuple-element.256, f32[128,8,1152]{2,0,1:T(8,128)} %fusion.169, bf16[4,128,8,128]{1,3,2,0:T(8,128)(2,1)} %get-tuple-element.274, f32[128,8,1152]{2,0,1:T(8,128)} %get-tuple-element.242, ...), kind=kOutput, calls=%fused_computation.17.clone.1 | convolution fusion | flops 310249600 | bytes 19735552 | tf_op jit(solution)/shard_map/while/body/eval_jaxpr/rhk,rhd->kd/dot_general | solution.py:55
  449.0 12.5 %fusion.170 = bf16[4,128,8,128]{3,1,2,0:T(8,128)(2,1)} fusion(bf16[4,128,8,128]{3,1,2,0:T(8,128)(2,1)} %get-tuple-element.258, s32[]{:T(128)} %get-tuple-element.256, f32[128,8,1152]{2,0,1:T(8,128)} %fusion.169, bf16[4,1152,128]{2,1,0:T(8,128)(2,1)} %get-tuple-element.275, f32[128,8,1152]{2,0,1:T(8,128)} %get-tuple-element.242, ...), kind=kOutput, calls=%fused_computation.28.clone.1 | convolution fusion | flops 310380672 | bytes 19440640 | tf_op jit(solution)/shard_map/while/body/eval_jaxpr/rhk,kd->rhd/dot_general | solution.py:52
  472.4 5.7 exponential_reduce_fusion.2
  482.1 12.1 %fusion.171 = f32[4,1152,128]{1,2,0:T(8,128)S(1)} fusion(f32[4,1152,128]{1,2,0:T(8,128)S(1)} %get-tuple-element.259, s32[]{:T(128)} %get-tuple-element.256, f32[128,8,1152]{2,0,1:T(8,128)} %fusion.169, bf16[4,128,8,128]{1,3,2,0:T(8,128)(2,1)} %get-tuple-element.274, f32[128,8,1152]{2,0,1:T(8,128)} %get-tuple-element.242, ...), kind=kOutput, calls=%fused_computation.17.clone.1 | convolution fusion | flops 310249600 | bytes 19735552 | tf_op jit(solution)/shard_map/while/body/eval_jaxpr/rhk,rhd->kd/dot_general | solution.py:55
  494.2 12.5 %fusion.170 = bf16[4,128,8,128]{3,1,2,0:T(8,128)(2,1)} fusion(bf16[4,128,8,128]{3,1,2,0:T(8,128)(2,1)} %get-tuple-element.258, s32[]{:T(128)} %get-tuple-element.256, f32[128,8,1152]{2,0,1:T(8,128)} %fusion.169, bf16[4,1152,128]{2,1,0:T(8,128)(2,1)} %get-tuple-element.275, f32[128,8,1152]{2,0,1:T(8,128)} %get-tuple-element.242, ...), kind=kOutput, calls=%fused_computation.28.clone.1 | convolution fusion | flops 310380672 | bytes 19440640 | tf_op jit(solution)/shard_map/while/body/eval_jaxpr/rhk,kd->rhd/dot_general | solution.py:52
  525.2 5.8 collective-permute-start.12
  536.8 17.9 %collective-permute-start.15 = (f32[128,1024]{0,1:T(8,128)S(1)}, f32[128,1024]{0,1:T(8,128)S(1)}, u32[]{:S(2)}, u32[]{:S(2)}) collective-permute-start(f32[128,1024]{0,1:T(8,128)S(1)} %get-tuple-element.160), channel_id=1, source_target_pairs={{8,0},{9,1},{10,2},{11,3},{12,4},{13,5},{14,6},{15,7},{16,8},{17,9... | collective-permute-start | bytes 1572872 | tf_op jit(solution)/shard_map/ppermute | solution.py:28
  554.7 15.7 %collective-permute-done.11 = f32[128,1024]{0,1:T(8,128)S(1)} collective-permute-done((f32[128,1024]{0,1:T(8,128)S(1)}, f32[128,1024]{0,1:T(8,128)S(1)}, u32[]{:S(2)}, u32[]{:S(2)}) %collective-permute-start.11) | collective-permute-done | bytes 524320 | tf_op jit(solution)/shard_map/ppermute | solution.py:28
  570.5 17.8 %collective-permute-start.8 = (f32[128,1024]{0,1:T(8,128)S(1)}, f32[128,1024]{0,1:T(8,128)S(1)}, u32[]{:S(2)}, u32[]{:S(2)}) collective-permute-start(f32[128,1024]{0,1:T(8,128)S(1)} %get-tuple-element.154), channel_id=1, source_target_pairs={{1,0},{2,1},{3,2},{4,3},{5,4},{6,5},{7,6},{8,7},{9,8},{10,9},{11,1... | collective-permute-start | bytes 1572872 | tf_op jit(solution)/shard_map/ppermute | solution.py:28
  588.3 13.7 %collective-permute-start.9 = (f32[128,1024]{0,1:T(8,128)S(1)}, f32[128,1024]{0,1:T(8,128)S(1)}, u32[]{:S(2)}, u32[]{:S(2)}) collective-permute-start(f32[128,1024]{0,1:T(8,128)S(1)} %get-tuple-element.155), channel_id=1, source_target_pairs={{2,0},{3,1},{4,2},{5,3},{6,4},{7,5},{8,6},{9,7},{10,8},{11,9},{12,... | collective-permute-start | bytes 1572872 | tf_op jit(solution)/shard_map/ppermute | solution.py:28
  602.0 32.7 %collective-permute-done.13 = f32[128,1024]{0,1:T(8,128)S(1)} collective-permute-done((f32[128,1024]{0,1:T(8,128)S(1)}, f32[128,1024]{0,1:T(8,128)S(1)}, u32[]{:S(2)}, u32[]{:S(2)}) %collective-permute-start.13) | collective-permute-done | bytes 524320 | tf_op jit(solution)/shard_map/ppermute | solution.py:28
  634.7 7.5 collective-permute-done.14
  649.5 131.0 %all_to_all.19 = bf16[128,16,512]{0,2,1:T(8,128)(2,1)} all-to-all(bf16[128,16,512]{0,2,1:T(8,128)(2,1)} %bitcast.168), channel_id=1, replica_groups=mesh['seq'=16,'fsdp_0'=8,'fsdp_1'=2] {'fsdp_0','fsdp_1'}, dimensions={1} | all-to-all | bytes 4194304 | tf_op jit(solution)/shard_map/all_to_all | solution.py:86
  784.4 56.0 %all-gather.8.cloned.1.call-done = bf16[2048,1024]{0,1:T(8,128)(2,1)} async-done(((bf16[128,1024]{0,1:T(8,128)(2,1)}), bf16[2048,1024]{0,1:T(8,128)(2,1)}) %all-gather.8.cloned.1.call-update) | async-done | bytes 4194320 | tf_op jit(solution)/shard_map/all_gather | solution.py:117
  840.5 6.5 convolution_bitcast_fusion.2
  852.6 13.9 %convolution_convert_fusion.1 = bf16[128,8192]{1,0:T(8,128)(2,1)} fusion(bf16[8192,1024]{1,0:T(8,128)(2,1)} %all-gather.6.cloned.1.call-done, f32[128,1024]{0,1:T(8,128)} %copy-done.5, f32[128,1024]{0,1:T(8,128)} %copy-done.4, f32[128,1024]{0,1:T(8,128)} %copy-done.3, f32[128,1024]{0,1:T(8,128)} %copy-done.2, f32[128,1024]{0,1:T(8,128)S(1)} %collective-permute-done.11, ...), kind=kOutput, calls=%fused_computation.83 | convolution fusion | flops 2150891520 | bytes 27787272 | tf_op jit(solution)/shard_map/dot_general | solution.py:112
  866.5 136.3 %all-reduce.2.cloned.1.call-done = f32[512,1024]{0,1:T(8,128)} async-done(((f32[512,1024]{0,1:T(8,128)}), f32[512,1024]{0,1:T(8,128)}) %all-reduce.2.cloned.1.call-update) | async-done | bytes 2097168 | tf_op jit(solution)/shard_map/psum | solution.py:121
  (96 shorter events, 140.9 us)
Async XLA Ops:
  7.2 1.2 copy-start.9
  7.2 45.2 %all-gather.4.cloned.1.call-start = ((), (), s32[]{:S(2)}) async-start(), calls=%async_computation.1 | async-start | bytes 3145728 | tf_op jit(solution)/shard_map/all_gather | solution.py:21
  10.0 218.0 %copy-start.1 = (bf16[128,8192]{1,0:T(8,128)(2,1)S(1)}, bf16[128,8192]{1,0:T(8,128)(2,1)}, u32[]{:S(2)}) copy-start(bf16[128,8192]{1,0:T(8,128)(2,1)} %param.7) | copy-start | bytes 6291460
  10.0 218.0 %all-gather.6.cloned.1.call-start = ((), (), s32[]{:S(2)}) async-start(), calls=%async_computation.2 | async-start | bytes 18874368 | tf_op jit(solution)/shard_map/all_gather | solution.py:21
  52.4 788.0 %all-gather.8.cloned.1.call-start = ((), (), s32[]{:S(2)}) async-start(), calls=%async_computation.3 | async-start | bytes 4456448 | tf_op jit(solution)/shard_map/all_gather | solution.py:117
  236.1 26.6 %collective-permute-start = (bf16[128,1024]{1,0:T(8,128)(2,1)S(1)}, bf16[128,1024]{1,0:T(8,128)(2,1)}, u32[]{:S(2)}, u32[]{:S(2)}) collective-permute-start(bf16[128,1024]{1,0:T(8,128)(2,1)S(1)} %fusion.100), channel_id=1, source_target_pairs={{0,8},{1,9},{2,10},{3,11},{4,12},{5,13},{6,14},{7,15},{8,16},{9,17... | collective-permute-start | bytes 786440 | tf_op jit(solution)/shard_map/ppermute | solution.py:28
  240.8 28.2 %collective-permute-start.1 = (bf16[128,1024]{1,0:T(8,128)(2,1)S(1)}, bf16[128,1024]{1,0:T(8,128)(2,1)S(1)}, u32[]{:S(2)}, u32[]{:S(2)}) collective-permute-start(bf16[128,1024]{1,0:T(8,128)(2,1)S(1)} %fusion.100), channel_id=1, source_target_pairs={{0,7},{1,8},{2,9},{3,10},{4,11},{5,12},{6,13},{7,14},{8,15},{9,16}... | collective-permute-start | bytes 786440 | tf_op jit(solution)/shard_map/ppermute | solution.py:28
  245.0 45.6 %collective-permute-start.2 = (bf16[128,1024]{1,0:T(8,128)(2,1)S(1)}, bf16[128,1024]{1,0:T(8,128)(2,1)S(1)}, u32[]{:S(2)}, u32[]{:S(2)}) collective-permute-start(bf16[128,1024]{1,0:T(8,128)(2,1)S(1)} %fusion.100), channel_id=1, source_target_pairs={{0,6},{1,7},{2,8},{3,9},{4,10},{5,11},{6,12},{7,13},{8,14},{9,15},... | collective-permute-start | bytes 786440 | tf_op jit(solution)/shard_map/ppermute | solution.py:28
  255.4 50.2 %collective-permute-start.3 = (bf16[128,1024]{1,0:T(8,128)(2,1)S(1)}, bf16[128,1024]{1,0:T(8,128)(2,1)S(1)}, u32[]{:S(2)}, u32[]{:S(2)}) collective-permute-start(bf16[128,1024]{1,0:T(8,128)(2,1)S(1)} %fusion.100), channel_id=1, source_target_pairs={{0,5},{1,6},{2,7},{3,8},{4,9},{5,10},{6,11},{7,12},{8,13},{9,14},{... | collective-permute-start | bytes 786440 | tf_op jit(solution)/shard_map/ppermute | solution.py:28
  260.3 45.2 %collective-permute-start.4 = (bf16[128,1024]{1,0:T(8,128)(2,1)S(1)}, bf16[128,1024]{1,0:T(8,128)(2,1)S(1)}, u32[]{:S(2)}, u32[]{:S(2)}) collective-permute-start(bf16[128,1024]{1,0:T(8,128)(2,1)S(1)} %fusion.100), channel_id=1, source_target_pairs={{0,4},{1,5},{2,6},{3,7},{4,8},{5,9},{6,10},{7,11},{8,12},{9,13},{1... | collective-permute-start | bytes 786440 | tf_op jit(solution)/shard_map/ppermute | solution.py:28
  262.7 50.7 %collective-permute-start.5 = (bf16[128,1024]{1,0:T(8,128)(2,1)S(1)}, bf16[128,1024]{1,0:T(8,128)(2,1)S(1)}, u32[]{:S(2)}, u32[]{:S(2)}) collective-permute-start(bf16[128,1024]{1,0:T(8,128)(2,1)S(1)} %fusion.100), channel_id=1, source_target_pairs={{0,3},{1,4},{2,5},{3,6},{4,7},{5,8},{6,9},{7,10},{8,11},{9,12},{10... | collective-permute-start | bytes 786440 | tf_op jit(solution)/shard_map/ppermute | solution.py:28
  269.0 52.8 %collective-permute-start.6 = (bf16[128,1024]{1,0:T(8,128)(2,1)S(1)}, bf16[128,1024]{1,0:T(8,128)(2,1)S(1)}, u32[]{:S(2)}, u32[]{:S(2)}) collective-permute-start(bf16[128,1024]{1,0:T(8,128)(2,1)S(1)} %fusion.100), channel_id=1, source_target_pairs={{0,2},{1,3},{2,4},{3,5},{4,6},{5,7},{6,8},{7,9},{8,10},{9,11},{10,... | collective-permute-start | bytes 786440 | tf_op jit(solution)/shard_map/ppermute | solution.py:28
  290.5 43.6 %collective-permute-start.7 = (bf16[128,1024]{1,0:T(8,128)(2,1)S(1)}, bf16[128,1024]{1,0:T(8,128)(2,1)S(1)}, u32[]{:S(2)}, u32[]{:S(2)}) collective-permute-start(bf16[128,1024]{1,0:T(8,128)(2,1)S(1)} %fusion.100), channel_id=1, source_target_pairs={{0,1},{1,2},{2,3},{3,4},{4,5},{5,6},{6,7},{7,8},{8,9},{9,10},{10,1... | collective-permute-start | bytes 786440 | tf_op jit(solution)/shard_map/ppermute | solution.py:28
  516.7 127.6 %copy-start = (f32[4,1152,128]{1,2,0:T(8,128)S(1)}, f32[4,1152,128]{1,2,0:T(8,128)}, u32[]{:S(2)}) copy-start(f32[4,1152,128]{1,2,0:T(8,128)} %get-tuple-element.62) | copy-start | bytes 7077892
  518.7 18.1 %collective-permute-start.10 = (f32[128,1024]{0,1:T(8,128)S(1)}, f32[128,1024]{0,1:T(8,128)S(1)}, u32[]{:S(2)}, u32[]{:S(2)}) collective-permute-start(f32[128,1024]{0,1:T(8,128)S(1)} %get-tuple-element.156), channel_id=1, source_target_pairs={{3,0},{4,1},{5,2},{6,3},{7,4},{8,5},{9,6},{10,7},{11,8},{12,9},{13... | collective-permute-start | bytes 1572872 | tf_op jit(solution)/shard_map/ppermute | solution.py:28
  520.6 49.9 %collective-permute-start.11 = (f32[128,1024]{0,1:T(8,128)S(1)}, f32[128,1024]{0,1:T(8,128)S(1)}, u32[]{:S(2)}, u32[]{:S(2)}) collective-permute-start(f32[128,1024]{0,1:T(8,128)S(1)} %get-tuple-element.157), channel_id=1, source_target_pairs={{4,0},{5,1},{6,2},{7,3},{8,4},{9,5},{10,6},{11,7},{12,8},{13,9},{1... | collective-permute-start | bytes 1572872 | tf_op jit(solution)/shard_map/ppermute | solution.py:28
  525.2 63.1 %collective-permute-start.12 = (f32[128,1024]{0,1:T(8,128)S(1)}, f32[128,1024]{0,1:T(8,128)S(1)}, u32[]{:S(2)}, u32[]{:S(2)}) collective-permute-start(f32[128,1024]{0,1:T(8,128)S(1)} %get-tuple-element.158), channel_id=1, source_target_pairs={{5,0},{6,1},{7,2},{8,3},{9,4},{10,5},{11,6},{12,7},{13,8},{14,9},{... | collective-permute-start | bytes 1572872 | tf_op jit(solution)/shard_map/ppermute | solution.py:28
  531.0 103.8 %collective-permute-start.13 = (f32[128,1024]{0,1:T(8,128)S(1)}, f32[128,1024]{0,1:T(8,128)S(1)}, u32[]{:S(2)}, u32[]{:S(2)}) collective-permute-start(f32[128,1024]{0,1:T(8,128)S(1)} %get-tuple-element.159), channel_id=1, source_target_pairs={{6,0},{7,1},{8,2},{9,3},{10,4},{11,5},{12,6},{13,7},{14,8},{15,9},... | collective-permute-start | bytes 1572872 | tf_op jit(solution)/shard_map/ppermute | solution.py:28
  533.0 109.3 %collective-permute-start.14 = (f32[128,1024]{0,1:T(8,128)S(1)}, f32[128,1024]{0,1:T(8,128)S(1)}, u32[]{:S(2)}, u32[]{:S(2)}) collective-permute-start(f32[128,1024]{0,1:T(8,128)S(1)} %get-tuple-element.161), channel_id=1, source_target_pairs={{7,0},{8,1},{9,2},{10,3},{11,4},{12,5},{13,6},{14,7},{15,8},{16,9}... | collective-permute-start | bytes 1572872 | tf_op jit(solution)/shard_map/ppermute | solution.py:28
  536.8 105.5 %collective-permute-start.15 = (f32[128,1024]{0,1:T(8,128)S(1)}, f32[128,1024]{0,1:T(8,128)S(1)}, u32[]{:S(2)}, u32[]{:S(2)}) collective-permute-start(f32[128,1024]{0,1:T(8,128)S(1)} %get-tuple-element.160), channel_id=1, source_target_pairs={{8,0},{9,1},{10,2},{11,3},{12,4},{13,5},{14,6},{15,7},{16,8},{17,9... | collective-permute-start | bytes 1572872 | tf_op jit(solution)/shard_map/ppermute | solution.py:28
  570.5 71.8 %collective-permute-start.8 = (f32[128,1024]{0,1:T(8,128)S(1)}, f32[128,1024]{0,1:T(8,128)S(1)}, u32[]{:S(2)}, u32[]{:S(2)}) collective-permute-start(f32[128,1024]{0,1:T(8,128)S(1)} %get-tuple-element.154), channel_id=1, source_target_pairs={{1,0},{2,1},{3,2},{4,3},{5,4},{6,5},{7,6},{8,7},{9,8},{10,9},{11,1... | collective-permute-start | bytes 1572872 | tf_op jit(solution)/shard_map/ppermute | solution.py:28
  588.3 54.0 %copy-start.2 = (f32[128,1024]{0,1:T(8,128)}, f32[128,1024]{0,1:T(8,128)S(1)}, u32[]{:S(2)}) copy-start(f32[128,1024]{0,1:T(8,128)S(1)} %collective-permute-done.12) | copy-start | bytes 1572868
  588.3 54.0 %collective-permute-start.9 = (f32[128,1024]{0,1:T(8,128)S(1)}, f32[128,1024]{0,1:T(8,128)S(1)}, u32[]{:S(2)}, u32[]{:S(2)}) collective-permute-start(f32[128,1024]{0,1:T(8,128)S(1)} %get-tuple-element.155), channel_id=1, source_target_pairs={{2,0},{3,1},{4,2},{5,3},{6,4},{7,5},{8,6},{9,7},{10,8},{11,9},{12,... | collective-permute-start | bytes 1572872 | tf_op jit(solution)/shard_map/ppermute | solution.py:28
  634.7 7.6 copy-start.3
  642.3 0.8 copy-start.4
  642.3 1.0 copy-start.5
  642.3 1.2 copy-start.6
  643.5 0.8 copy-start.7
  645.4 357.4 %all-reduce.2.cloned.1.call-start = ((), (), s32[]{:S(2)}) async-start(), calls=%async_computation.4 | async-start | bytes 4194304 | tf_op jit(solution)/shard_map/psum | solution.py:121
  847.0 3.4 copy-start.8
Sparse Core Ops, SparseCore 0:
  10.4 41.9 all-gather.3
  54.2 173.7 all-gather.5
  645.5 194.9 all-gather.7
  847.1 155.5 all-reduce.1
where the time goes:
time: 1010 us
  waiting for transfers between devices  529 us (52%)
  matrix products  206 us (20%)
  blocking collectives  131 us (13%)
  starting transfers between devices  97.6 us (10%)
  local copies, waits for them, and re-layouts  27.1 us (3%)
  between operations  14.2 us (1%)
    all_gather x2, waiting for transfers between devices, gather_axes(): nearer = lax.all_gather(value, axes[-1], axis=dim, tiled=True)  218 us
    psum x1, waiting for transfers between devices, body(): weight_grad = lax.psum(shard_grad, 'seq')  136 us
    all_to_all x1, blocking collectives, body(): lax.all_to_all(hidden, FSDP, split_axis=1, concat_axis=0, tiled=True)  131 us
    ppermute x16, waiting for transfers between devices, shifted(): return lax.ppermute(block, axis, route)  118 us
    ppermute x16, starting transfers between devices, shifted(): return lax.ppermute(block, axis, route)  97.5 us
    all_gather x1, waiting for transfers between devices, body(): lax.all_gather(all_grad, FSDP, axis=0, tiled=True)  56 us
    dot_general x4, matrix products, attend_group(): jnp.einsum('rhk,kd->rhd', dscores, kgrp, preferred_element_type=jnp.float32)  50.1 us
    dot_general x4, matrix products, attend_group(): jnp.einsum('rhk,rhd->kd', dscores, qgrp, preferred_element_type=jnp.float32)  48.3 us
  transfers between devices with their start and end apart: 20, of which 13 were waited for; matrix products, arithmetic and copies ran while one was open for 3% of the time, Pallas kernels for 0%

commit v1 on v0

v1 whole, which is shorter than its diff:
```python
import functools

import jax
import jax.numpy as jnp
from jax import lax
from jax.experimental import pallas as pl
from jax.experimental.pallas import tpu as pltpu
from jax.sharding import Mesh
from jax.sharding import PartitionSpec as P

HEADS = 32
KV_HEADS = 4
HEAD = 128
QB = 128
SPAN = 1024
AXES = ("x", "yh", "core", "zh", "zl", "yl")
SIZES = (4, 2, 2, 4, 2, 2)
FSDP = ("zh", "zl", "yl")
GROUP = ("zl", "yl")
PLANE = ("x", "yh")
MEMBERS = 4

FACTOR = 1.0 / float(HEAD) ** 0.5
LOG2E = 1.4426950408889634
NEG = -1e30
F32 = jnp.float32
BF16 = jnp.bfloat16


def nt(a, b):
    return lax.dot_general(a, b, (((1,), (1,)), ((), ())), preferred_element_type=F32)


def nn(a, b):
    return lax.dot_general(a, b, (((1,), (0,)), ((), ())), preferred_element_type=F32)


def tn(a, b):
    return lax.dot_general(a, b, (((0,), (0,)), ((), ())), preferred_element_type=F32)


def shifted(block, axes, distance):
    devices = range(lax.axis_size(axes))
    route = [(i - distance, i) for i in devices if i - distance in devices]
    return lax.ppermute(block, axes, route)


def rotated(block, axis, distance):
    size = lax.axis_size(axis)
    return lax.ppermute(block, axis, [(i, (i + distance) % size) for i in range(size)])


def swapped(block, axes, mask):
    return lax.ppermute(block, axes, [(i, i ^ mask) for i in range(lax.axis_size(axes))])


def exchange(blocks, axes):
    return lax.all_to_all(blocks, axes, split_axis=0, concat_axis=0, tiled=True)


def dequantize(blocks, scale):
    rows, cols = blocks.shape
    grid = blocks.astype(F32).reshape(scale.shape[0], QB, scale.shape[1], QB)
    return (grid * scale[:, None, :, None]).reshape(rows, cols).astype(BF16)


def project_kernel(h_ref, w_ref, o_ref):
    o_ref[0] = nn(h_ref[...], w_ref[...])


def project(hidden, weights):
    rows, depth = hidden.shape
    width = weights.shape[1] // MEMBERS
    return pl.pallas_call(
        project_kernel,
        grid=(MEMBERS,),
        in_specs=[
            pl.BlockSpec((rows, depth), lambda h: (0, 0)),
            pl.BlockSpec((depth, width), lambda h: (0, h)),
        ],
        out_specs=pl.BlockSpec((1, rows, width), lambda h: (h, 0, 0)),
        out_shape=jax.ShapeDtypeStruct((MEMBERS, rows, width), F32),
        compiler_params=pltpu.CompilerParams(vmem_limit_bytes=32 << 20),
        cost_estimate=pl.CostEstimate(
            flops=2 * rows * depth * width * MEMBERS, bytes_accessed=8 << 20, transcendentals=0
        ),
        name="project",
    )(hidden, weights)


def attention_kernel(
    lim_ref, q_ref, g_ref, far_ref, near_ref, own_ref,
    out_ref, dfar_ref, dnear_ref, down_ref, kv, acc,
):
    t = pl.program_id(0)
    group = own_ref.shape[0]
    tok = q_ref.shape[2]
    pairs = q_ref.shape[3] // (2 * HEAD)
    width = SPAN + tok

    @pl.when(t == 0)
    def _():
        kv[0:group] = far_ref[...]
        kv[group : 2 * group] = near_ref[...]
        kv[2 * group :] = own_ref[...]
        acc[...] = jnp.zeros_like(acc)

    start = pl.multiple_of(t * tok, tok)
    lim = lim_ref[t]

    def run(masked):
        keys = kv[pl.ds(start, width), 0:HEAD]
        vals = kv[pl.ds(start, width), HEAD : 2 * HEAD]
        row = lax.broadcasted_iota(jnp.int32, (tok, 2 * tok), 0)
        col = lax.broadcasted_iota(jnp.int32, (tok, 2 * tok), 1) & (tok - 1)
        for pair in range(pairs):
            a = slice(2 * pair * HEAD, (2 * pair + 1) * HEAD)
            b = slice((2 * pair + 1) * HEAD, (2 * pair + 2) * HEAD)
            q2 = jnp.concatenate([q_ref[0, 0, :, a], q_ref[0, 0, :, b]], axis=0)
            g2 = jnp.concatenate([g_ref[0, 0, :, a], g_ref[0, 0, :, b]], axis=0)
            s = nt(keys, q2)
            s = jnp.concatenate(
                [
                    jnp.where(row > col, s[:tok], NEG),
                    s[tok:SPAN],
                    jnp.where(row <= col, s[SPAN:], NEG),
                ],
                axis=0,
            )
            if masked:
                s = jnp.where(lax.broadcasted_iota(jnp.int32, s.shape, 0) >= lim, s, NEG)
            top = jnp.max(s, axis=0, keepdims=True) * (FACTOR * LOG2E)
            expd = jnp.exp2(s * (FACTOR * LOG2E) - top)
            probs = expd * (1.0 / jnp.sum(expd, axis=0, keepdims=True))
            probs_b = probs.astype(BF16)
            dprobs = nt(vals, g2)
            delta = jnp.sum(probs * dprobs, axis=0, keepdims=True)
            dscores = (probs * (dprobs - delta) * FACTOR).astype(BF16)
            acc[pl.ds(start, width), 0:HEAD] += nn(dscores, q2)
            acc[pl.ds(start, width), HEAD : 2 * HEAD] += nn(probs_b, g2)
            output = tn(probs_b, vals).astype(BF16)
            gradq = tn(dscores, keys).astype(BF16)
            out_ref[0, 0, :, a] = output[:tok]
            out_ref[0, 0, :, b] = output[tok:]
            out_ref[0, 1, :, a] = gradq[:tok]
            out_ref[0, 1, :, b] = gradq[tok:]

    @pl.when(lim <= 0)
    def _():
        run(False)

    @pl.when(lim > 0)
    def _():
        run(True)

    @pl.when(t == pl.num_programs(0) - 1)
    def _():
        dfar_ref[...] = acc[0:group].astype(dfar_ref.dtype)
        dnear_ref[...] = acc[group : 2 * group].astype(dnear_ref.dtype)
        down_ref[...] = acc[2 * group :]


def attention(lim, queries, far, near, own):
    steps, _, tok, cols = queries.shape
    group, both = own.shape
    whole = pl.BlockSpec((group, both), lambda t, lim: (0, 0))
    return pl.pallas_call(
        attention_kernel,
        grid_spec=pltpu.PrefetchScalarGridSpec(
            num_scalar_prefetch=1,
            grid=(steps,),
            in_specs=[
                pl.BlockSpec((1, 1, tok, cols), lambda t, lim: (t, 0, 0, 0)),
                pl.BlockSpec((1, 1, tok, cols), lambda t, lim: (t, 1, 0, 0)),
                whole,
                whole,
                whole,
            ],
            out_specs=[
                pl.BlockSpec((1, 2, tok, cols), lambda t, lim: (t, 0, 0, 0)),
                whole,
                whole,
                whole,
            ],
            scratch_shapes=[
                pltpu.VMEM((3 * group, both), BF16),
                pltpu.VMEM((3 * group, both), F32),
            ],
        ),
        out_shape=[
            jax.ShapeDtypeStruct(queries.shape, BF16),
            jax.ShapeDtypeStruct(own.shape, BF16),
            jax.ShapeDtypeStruct(own.shape, BF16),
            jax.ShapeDtypeStruct(own.shape, F32),
        ],
        compiler_params=pltpu.CompilerParams(vmem_limit_bytes=48 << 20),
        cost_estimate=pl.CostEstimate(
            flops=30_000_000_000, bytes_accessed=6 << 20, transcendentals=5_000_000
        ),
        name="attention",
    )(lim, queries, queries, far, near, own)


def grad_hidden_kernel(member_ref, d0, d1, d2, d3, w_ref, o_ref):
    total = None
    for k, d in enumerate((d0, d1, d2, d3)):
        width = d.shape[1]
        at = pl.multiple_of((member_ref[0] ^ k) * width, width)
        term = nt(d[...], w_ref[:, pl.ds(at, width)])
        total = term if total is None else total + term
    o_ref[...] = total.astype(BF16)


def grad_hidden_quarter(member, pieces, weights):
    rows, width = pieces[0].shape
    depth, cols = weights.shape
    step = 256
    piece = pl.BlockSpec((rows, width), lambda i, m: (0, 0))
    return pl.pallas_call(
        grad_hidden_kernel,
        grid_spec=pltpu.PrefetchScalarGridSpec(
            num_scalar_prefetch=1,
            grid=(depth // step,),
            in_specs=[piece] * 4 + [pl.BlockSpec((step, cols), lambda i, m: (i, 0))],
            out_specs=pl.BlockSpec((rows, step), lambda i, m: (0, i)),
        ),
        out_shape=jax.ShapeDtypeStruct((rows, depth), BF16),
        compiler_params=pltpu.CompilerParams(vmem_limit_bytes=32 << 20),
        cost_estimate=pl.CostEstimate(
            flops=2 * rows * depth * cols, bytes_accessed=8 << 20, transcendentals=0
        ),
        name="grad_hidden",
    )(member, *pieces, weights)


def weight_grad_kernel(place_ref, c0, c1, c2, c3, d_ref, o_ref):
    zh = place_ref[0]
    total = None
    for k, c in enumerate((c0, c1, c2, c3)):
        term = nn(c[...], d_ref[(zh - k) & 3, 0, 0])
        total = term if total is None else total + term
    h = pl.program_id(0)
    half = o_ref.shape[1] // 2
    at = pl.multiple_of(h * HEAD, HEAD)
    o_ref[:, pl.ds(at, HEAD)] = total[:, :HEAD]
    o_ref[:, pl.ds(half + at, HEAD)] = total[:, HEAD:]


def weight_grad_share(place, columns, gathered):
    feats, rows = columns[0].shape
    blocks = gathered.shape[0]
    both = gathered.shape[4]
    piece = pl.BlockSpec((feats, rows), lambda h, p: (0, 0))
    return pl.pallas_call(
        weight_grad_kernel,
        grid_spec=pltpu.PrefetchScalarGridSpec(
            num_scalar_prefetch=1,
            grid=(KV_HEADS,),
            in_specs=[piece] * 4
            + [
                pl.BlockSpec(
                    (blocks, 1, 1, rows, both), lambda h, p: (0, h // 2, (h % 2) ^ p[1], 0, 0)
                )
            ],
            out_specs=pl.BlockSpec((feats, both * KV_HEADS), lambda h, p: (0, 0)),
        ),
        out_shape=jax.ShapeDtypeStruct((feats, both * KV_HEADS), F32),
        compiler_params=pltpu.CompilerParams(vmem_limit_bytes=32 << 20),
        cost_estimate=pl.CostEstimate(
            flops=2 * feats * rows * blocks * both * KV_HEADS,
            bytes_accessed=8 << 20,
            transcendentals=0,
        ),
        name="weight_grad",
    )(place, *columns, gathered)


def body(hidden, kv_blocks, kv_scale, queries, grad_out):
    tok, depth = hidden.shape
    shard = kv_blocks.shape[0]
    half = shard // 2
    kv_cols = kv_blocks.shape[1]
    group = MEMBERS * tok
    zh = lax.axis_index("zh")
    core = lax.axis_index("core")
    yl = lax.axis_index("yl")
    member = lax.axis_index(GROUP)
    zhs = lax.axis_size("zh")

    blocks = lax.dynamic_slice_in_dim(kv_blocks, core * half, half, 0)
    scale = lax.dynamic_slice_in_dim(kv_scale, core * (half // QB), half // QB, 0)
    rows = dequantize(blocks, scale)
    rows = rows.reshape(half, 2, KV_HEADS, HEAD).transpose(0, 2, 1, 3).reshape(half, kv_cols)
    weights = lax.all_gather(rows, ("core", "zh"), axis=0, tiled=True)

    quarters = (
        hidden.reshape(tok, zhs, MEMBERS, 2, half).transpose(2, 0, 3, 1, 4).reshape(group, -1)
    )
    quarter = exchange(quarters, GROUP)

    pieces = jnp.stack(
        [
            queries.reshape(tok, MEMBERS, -1).transpose(1, 0, 2),
            grad_out.reshape(tok, MEMBERS, -1).transpose(1, 0, 2),
        ],
        axis=1,
    )
    heads = exchange(pieces, GROUP)

    partial = exchange(project(quarter, weights), GROUP)
    own = jnp.sum(partial, axis=0).astype(BF16)
    far = shifted(own, AXES, 2 * MEMBERS)
    near = shifted(own, AXES, MEMBERS)

    first = lax.axis_index(AXES) // MEMBERS * MEMBERS
    lim = jnp.maximum(0, SPAN - (first + jnp.arange(MEMBERS, dtype=jnp.int32)) * tok)

    far, near, quarter = lax.optimization_barrier((far, near, quarter))
    grid = quarter.reshape(group, 2, zhs, half)
    columns = []
    for k in range(zhs):
        to = (zh + k) % zhs
        block = lax.dynamic_slice_in_dim(grid, to, 1, 2).reshape(group, shard)
        columns.append(rotated(block, "zh", k) if k else block)

    out, dfar, dnear, down = attention(lim, heads, far, near, own)
    from_far = shifted(dfar, AXES, -2 * MEMBERS).astype(F32)
    from_near = shifted(dnear, AXES, -MEMBERS).astype(F32)
    all_grad = (down + from_near + from_far).astype(BF16)
    inside = down + jnp.where(zh + 1 < zhs, from_near, 0.0) + jnp.where(zh + 2 < zhs, from_far, 0.0)
    seg_grad = inside.astype(BF16)

    other = swapped(all_grad, "yl", 1)
    pair = jnp.stack([all_grad, other], axis=0)[None]
    gathered = lax.all_gather(pair, ("zh", "zl"), axis=0, tiled=True)
    gathered = gathered.reshape(zhs, 2, 2, group, -1)

    out, seg_grad, _ = lax.optimization_barrier((out, seg_grad, pair))
    turned = [c.T for c in columns]
    segs = [seg_grad] + [swapped(seg_grad, GROUP, k) for k in (1, 2, 3)]
    back = exchange(grad_hidden_quarter(member.reshape(1), segs, weights), GROUP)
    grad_hidden = (
        back.reshape(MEMBERS, tok, 2, zhs, half).transpose(1, 3, 0, 2, 4).reshape(tok, depth)
    )
    out = exchange(out, GROUP)
    attn_out = out[:, 0].transpose(1, 0, 2).reshape(tok, -1)
    grad_queries = out[:, 1].transpose(1, 0, 2).reshape(tok, -1)

    share = weight_grad_share(jnp.stack([zh, yl]).astype(jnp.int32), turned, gathered)
    mine = lax.dynamic_slice_in_dim(share, core * half, half, 0)
    theirs = lax.dynamic_slice_in_dim(share, (1 - core) * half, half, 0)
    mine = mine + swapped(theirs, "core", 1)
    planes = lax.axis_size(PLANE)
    parts = exchange(mine.reshape(planes, half // planes, kv_cols), PLANE)
    summed = jnp.sum(parts, axis=0)
    spread = exchange(jnp.broadcast_to(summed[None], parts.shape), PLANE).reshape(half, kv_cols)
    opposite = swapped(spread, "core", 1)
    weight_grad = jnp.where(
        core == 0,
        jnp.concatenate([spread, opposite], axis=0),
        jnp.concatenate([opposite, spread], axis=0),
    )
    return (attn_out, grad_queries, grad_hidden, weight_grad)


def solution(mesh):
    finer = Mesh(mesh.devices.reshape(SIZES), AXES)
    placed = (P(AXES, None), P(FSDP, None), P(FSDP, None), P(AXES, None), P(AXES, None))
    return jax.shard_map(
        body,
        mesh=finer,
        in_specs=placed,
        out_specs=(P(AXES, None), P(AXES, None), P(AXES, None), P(FSDP, None)),
        check_vma=False,
    )
```

time: 1010 us -> 484 us (0.48)
  waiting for transfers between devices: 529 us -> 225 us
  matrix products: 206 us -> 0 us
  blocking collectives: 131 us -> 60.7 us
  Pallas kernels: 0 us -> 42.8 us
  local copies, waits for them, and re-layouts: 27.1 us -> 65.3 us
  starting transfers between devices: 97.6 us -> 60.7 us
    all_gather x3 -> x2, waiting for transfers between devices: 274 us -> 23.5 us  [the longest x1 18.4 us: body(): gathered = lax.all_gather(pair, ('zh', 'zl'), axis=0, tiled=True)]
    dot_general x23 -> x0, matrix products: 183 us -> none  [the longest x4 50.1 us: attend_group(): jnp.einsum('rhk,kd->rhd', dscores, kgrp, preferred_element_type=jnp.float32)]
    psum x1 -> x0, waiting for transfers between devices: 136 us -> none  [body(): weight_grad = lax.psum(shard_grad, 'seq')]
    all_to_all x0 -> x6, waiting for transfers between devices: none -> 71.9 us  [exchange(): return lax.all_to_all(blocks, axes, split_axis=0, concat_axis=0, tiled=True)]
    all_to_all x1, blocking collectives: 131 us -> 60.7 us  [exchange(): return lax.all_to_all(blocks, axes, split_axis=0, concat_axis=0, tiled=True)]
    ppermute x16 -> x13, starting transfers between devices: 97.5 us -> 31.6 us  [the longest x4 16.2 us: shifted(): return lax.ppermute(block, axes, route)]
    pallas_call x0 -> x4, Pallas kernels: none -> 42.8 us  [the longest x1 30.2 us: attention(): pl.pallas_call(attention_kernel, grid_spec=pltpu.PrefetchScalarGridSpec(n...]
    all_to_all x0 -> x6, starting transfers between devices: none -> 29.1 us  [exchange(): return lax.all_to_all(blocks, axes, split_axis=0, concat_axis=0, tiled=True)]
  transfers between devices with their start and end apart: 20 -> 21, of which waited for: 13 -> 15; matrix products, arithmetic and copies ran while one was open for 3% -> 11% of each run, Pallas kernels for 0% -> 1%
where the time goes in v1:
time: 484 us; the launch traced here: 481 us
  waiting for transfers between devices  225 us (46%)
  local copies, waits for them, and re-layouts  65.3 us (13%)
  starting transfers between devices  60.7 us (13%)
  blocking collectives  60.7 us (13%)
  Pallas kernels  42.8 us (9%)
  between operations  14.4 us (3%)
  other arithmetic  12.7 us (3%)
    all_to_all x6, waiting for transfers between devices, exchange(): return lax.all_to_all(blocks, axes, split_axis=0, concat_axis=0, tiled=True)  71.9 us
    all_to_all x1, blocking collectives, exchange(): return lax.all_to_all(blocks, axes, split_axis=0, concat_axis=0, tiled=True)  60.7 us
    ppermute x3, waiting for transfers between devices, rotated(): lax.ppermute(block, axis, [(i, (i + distance) % size) for i in range(size)])  54.7 us
    ppermute x4, waiting for transfers between devices, shifted(): return lax.ppermute(block, axes, route)  45 us
    pallas_call x1, Pallas kernels, attention(): pl.pallas_call(attention_kernel, grid_spec=pltpu.PrefetchScalarGridSpec(n...  30.2 us
    ppermute x6, waiting for transfers between devices, swapped(): lax.ppermute(block, axes, [(i, i ^ mask) for i in range(lax.axis_size(axe...  29.5 us
    all_to_all x6, starting transfers between devices, exchange(): return lax.all_to_all(blocks, axes, split_axis=0, concat_axis=0, tiled=True)  29.1 us
    unnamed x30, local copies, waits for them, and re-layouts  23.7 us
  transfers between devices with their start and end apart: 21, of which 15 were waited for; matrix products, arithmetic and copies ran while one was open for 11% of the time, Pallas kernels for 1%

profile of v1, /device:TPU:1, one launch (start us, length us, event | category | flops | bytes accessed | tf_op | source)
XLA Modules:
  0.0 481.3 jit_solution(6594527429235256154)
XLA Ops:
  19.7 60.7 %all_to_all.45 = bf16[4,128,2048]{2,1,0:T(8,128)(2,1)S(1)} all-to-all(bf16[4,128,2048]{2,1,0:T(8,128)(2,1)} %all_to_all.29), channel_id=1, replica_groups=mesh['x'=4,'yh'=2,'core'=2,'zh'=4,'zl'=2,'yl'=2] {'zl','yl'}, dimensions={0} | all-to-all | bytes 4194304 | tf_op jit(solution)/shard_map/all_to_all | solution.py:58
  80.3 5.2 %all-gather.4.cloned.1.call-done.w_ref = bf16[2048,1024]{1,0:T(8,128)(2,1)} async-done(((bf16[256,1024]{1,0:T(8,128)(2,1)}), bf16[2048,1024]{1,0:T(8,128)(2,1)}) %all-gather.4.cloned.1.call-update) | async-done | bytes 4194320 | tf_op jit(solution)/shard_map/all_gather | solution.py:294
  87.7 3.5 project.1
  92.5 4.5 all-to-all-start.2
  105.9 15.9 %all-to-all-done.2 = f32[4,512,256]{2,1,0:T(8,128)} async-done(((f32[4,512,256]{2,1,0:T(8,128)}), f32[4,512,256]{2,1,0:T(8,128)}, u32[]{:S(2)}, u32[]{:S(2)}) %all-to-all-start.2) | async-done | bytes 2097184 | tf_op jit(solution)/shard_map/all_to_all | solution.py:58
  121.8 4.4 all-to-all-start
  128.0 4.8 collective-permute-start
  132.8 4.2 collective-permute-start.1
  137.1 33.5 %collective-permute-done.far_ref = bf16[512,256]{1,0:T(8,128)(2,1)S(1)} collective-permute-done((bf16[512,256]{1,0:T(8,128)(2,1)S(1)}, bf16[512,256]{1,0:T(8,128)(2,1)S(1)}, u32[]{:S(2)}, u32[]{:S(2)}) %collective-permute-start) | collective-permute-done | bytes 262176 | tf_op jit(solution)/shard_map/ppermute | solution.py:45
  170.5 4.9 %collective-permute-done.1.near_ref = bf16[512,256]{1,0:T(8,128)(2,1)S(1)} collective-permute-done((bf16[512,256]{1,0:T(8,128)(2,1)S(1)}, bf16[512,256]{1,0:T(8,128)(2,1)S(1)}, u32[]{:S(2)}, u32[]{:S(2)}) %collective-permute-start.1) | collective-permute-done | bytes 262176 | tf_op jit(solution)/shard_map/ppermute | solution.py:45
  175.4 30.2 %attention.1 = (bf16[4,2,128,1024]{3,2,1,0:T(8,128)(2,1)}, bf16[512,256]{1,0:T(8,128)(2,1)}, bf16[512,256]{1,0:T(8,128)(2,1)}, f32[512,256]{1,0:T(8,128)S(1)}) custom-call(s32[4]{0:T(128)S(1)} %subtract_maximum_fusion.lim_ref, bf16[4,2,128,1024]{3,2,1,0:T(8,128)(2,1)} %all-to-all-done.q_ref.g_ref, bf16[4,2,128,1024]{3,2,1,0:T(8,128)(2,1)} %all-to-all-done.q_ref.g_ref, ...), custom_call_target="tpu_custom_call" | custom-call | flops 30000001024 | bytes 6291456 | tf_op jit(solution)/shard_map/attention/pallas_call | solution.py:167
  208.9 3.9 collective-permute-start.2
  212.8 6.1 %collective-permute-done.3 = bf16[512,256]{1,0:T(8,128)(2,1)S(1)} collective-permute-done((bf16[512,256]{1,0:T(8,128)(2,1)}, bf16[512,256]{1,0:T(8,128)(2,1)S(1)}, u32[]{:S(2)}, u32[]{:S(2)}) %collective-permute-start.3) | collective-permute-done | bytes 262176 | tf_op jit(solution)/shard_map/ppermute | solution.py:45
  222.5 6.6 %collective-permute-done.4 = bf16[512,256]{1,0:T(8,128)(2,1)S(1)} collective-permute-done((bf16[512,256]{1,0:T(8,128)(2,1)S(1)}, bf16[512,256]{1,0:T(8,128)(2,1)S(1)}, u32[]{:S(2)}, u32[]{:S(2)}) %collective-permute-start.4) | collective-permute-done | bytes 262176 | tf_op jit(solution)/shard_map/ppermute | solution.py:54
  232.9 9.0 %constant_dynamic-slice_fusion.1 = (bf16[512,2,1,256]{3,2,1,0:T(2,128)(2,1)S(1)}, bf16[512,2,1,256]{3,2,1,0:T(2,128)(2,1)S(1)}, bf16[512,2,1,256]{3,2,1,0:T(2,128)(2,1)S(1)}, bf16[512,2,1,256]{3,2,1,0:T(2,128)(2,1)}) fusion(bf16[512,2,4,256]{3,2,1,0:T(4,128)(2,1)} %reshape.84, s32[]{:T(128)S(6)} %select_n.82, s32[]{:T(128)S(6)} %select_n.80, ...), kind=kLoop, calls=%fused_computation.19 | loop fusion | bytes 4194320 | tf_op jit(solution)/shard_map/dynamic_slice | solution.py:323
  244.2 4.0 collective-permute-start.8
  258.9 25.5 %collective-permute-done.8 = bf16[512,512]{0,1:T(8,128)(2,1)S(1)} collective-permute-done((bf16[512,512]{0,1:T(8,128)(2,1)}, bf16[512,512]{0,1:T(8,128)(2,1)S(1)}, u32[]{:S(2)}, u32[]{:S(2)}) %collective-permute-start.8) | collective-permute-done | bytes 524320 | tf_op jit(solution)/shard_map/ppermute | solution.py:50
  284.4 29.1 %collective-permute-done.9 = bf16[512,512]{0,1:T(8,128)(2,1)S(1)} collective-permute-done((bf16[512,512]{0,1:T(8,128)(2,1)}, bf16[512,512]{0,1:T(8,128)(2,1)S(1)}, u32[]{:S(2)}, u32[]{:S(2)}) %collective-permute-start.9) | collective-permute-done | bytes 524320 | tf_op jit(solution)/shard_map/ppermute | solution.py:50
  313.5 18.4 %all-gather.6.cloned.1.call-done = bf16[16,512,256]{2,1,0:T(8,128)(2,1)} async-done(((bf16[2,512,256]{2,1,0:T(8,128)(2,1)}), bf16[16,512,256]{2,1,0:T(8,128)(2,1)}) %all-gather.6.cloned.1.call-update) | async-done | bytes 4194320 | tf_op jit(solution)/shard_map/all_gather | solution.py:335
  334.1 3.9 weight_grad.1
  342.1 7.8 %all-to-all-start.5 = ((f32[8,32,1024]{2,1,0:T(8,128)}), f32[8,32,1024]{2,1,0:T(8,128)S(1)}, u32[]{:S(2)}, u32[]{:S(2)}) async-start(f32[8,32,1024]{2,1,0:T(8,128)} %bitcast.31), calls=%async_computation.5 | async-start | bytes 2097152 | tf_op jit(solution)/shard_map/all_to_all | solution.py:58
  349.9 15.7 %all-to-all-done.5 = f32[8,32,1024]{2,1,0:T(8,128)S(1)} async-done(((f32[8,32,1024]{2,1,0:T(8,128)}), f32[8,32,1024]{2,1,0:T(8,128)S(1)}, u32[]{:S(2)}, u32[]{:S(2)}) %all-to-all-start.5) | async-done | bytes 1048608 | tf_op jit(solution)/shard_map/all_to_all | solution.py:58
  365.6 3.6 all-to-all-start.3
  369.3 24.2 %all-to-all-done.3 = bf16[4,2,128,1024]{3,2,1,0:T(8,128)(2,1)S(1)} async-done(((bf16[4,2,128,1024]{3,2,1,0:T(8,128)(2,1)}), bf16[4,2,128,1024]{3,2,1,0:T(8,128)(2,1)S(1)}, u32[]{:S(2)}, u32[]{:S(2)}) %all-to-all-start.3) | async-done | bytes 2097184 | tf_op jit(solution)/shard_map/all_to_all | solution.py:58
  395.2 4.2 all-to-all-start.6
  402.6 20.6 %collective-permute-done.5.d1 = bf16[512,256]{1,0:T(8,128)(2,1)S(1)} collective-permute-done((bf16[512,256]{1,0:T(8,128)(2,1)S(1)}, bf16[512,256]{1,0:T(8,128)(2,1)S(1)}, u32[]{:S(2)}, u32[]{:S(2)}) %collective-permute-start.5) | collective-permute-done | bytes 262176 | tf_op jit(solution)/shard_map/ppermute | solution.py:54
  425.4 5.2 %grad_hidden.1 = bf16[512,2048]{1,0:T(8,128)(2,1)} custom-call(s32[1]{0:T(128)} %bitcast.15.member_ref, bf16[512,256]{1,0:T(8,128)(2,1)S(1)} %get-tuple-element.20.d0, bf16[512,256]{1,0:T(8,128)(2,1)S(1)} %collective-permute-done.5.d1, bf16[512,256]{1,0:T(8,128)(2,1)S(1)} %collective-permute-done.6.d2, bf16[512,256]{1,0:T(8,128)(2,1)S(1)} %collective-permute-done.7.d3, ...), custom_call_target="tpu_custom_call" | custom-call | flops 2147483648 | bytes 8388608 | tf_op jit(solution)/shard_map/grad_hidden/pallas_call | solution.py:219
  430.6 4.6 all-to-all-start.4
  443.5 16.0 %all-to-all-done.4 = bf16[4,128,2048]{2,1,0:T(8,128)(2,1)} async-done(((bf16[4,128,2048]{2,1,0:T(8,128)(2,1)}), bf16[4,128,2048]{2,1,0:T(8,128)(2,1)}, u32[]{:S(2)}, u32[]{:S(2)}) %all-to-all-start.4) | async-done | bytes 2097184 | tf_op jit(solution)/shard_map/all_to_all | solution.py:58
  459.6 3.3 reshape.82
  462.9 3.8 copy.54
  466.7 4.5 reshape.83
  (77 shorter events, 75.0 us)
Async XLA Ops:
  7.2 0.7 copy-start
  7.2 78.3 %all-gather.4.cloned.1.call-start = ((), (), s32[]{:S(2)}) async-start(), calls=%async_computation.7 | async-start | bytes 4718592 | tf_op jit(solution)/shard_map/all_gather | solution.py:294
  9.7 1.7 copy-start.9
  85.5 2.2 copy-start.3
  91.2 1.3 copy-start.2
  92.5 29.3 %all-to-all-start.2 = ((f32[4,512,256]{2,1,0:T(8,128)}), f32[4,512,256]{2,1,0:T(8,128)}, u32[]{:S(2)}, u32[]{:S(2)}) async-start(f32[4,512,256]{2,1,0:T(8,128)} %copy-done.2), calls=%async_computation.2 | async-start | bytes 4194304 | tf_op jit(solution)/shard_map/all_to_all | solution.py:58
  121.8 53.7 %all-to-all-start = ((bf16[4,2,128,1024]{3,2,1,0:T(8,128)(2,1)}), bf16[4,2,128,1024]{3,2,1,0:T(8,128)(2,1)}, u32[]{:S(2)}, u32[]{:S(2)}) async-start(bf16[4,2,128,1024]{3,2,1,0:T(8,128)(2,1)} %pad_maximum_fusion), calls=%async_computation | async-start | bytes 4194304 | tf_op jit(solution)/shard_map/all_to_all | solution.py:58
  126.2 205.7 %all-gather.6.cloned.1.call-start = ((), (), s32[]{:S(2)}) async-start(), calls=%async_computation.8 | async-start | bytes 4718592 | tf_op jit(solution)/shard_map/all_gather | solution.py:335
  128.0 42.5 %collective-permute-start = (bf16[512,256]{1,0:T(8,128)(2,1)S(1)}, bf16[512,256]{1,0:T(8,128)(2,1)S(1)}, u32[]{:S(2)}, u32[]{:S(2)}) collective-permute-start(bf16[512,256]{1,0:T(8,128)(2,1)S(1)} %reduce_sum.18.own_ref), channel_id=1, source_target_pairs={{0,8},{1,9},{2,10},{3,11},{4,12},{5,13},{6,14},{7,15},{8,16},{9,17... | collective-permute-start | bytes 786440 | tf_op jit(solution)/shard_map/ppermute | solution.py:45
  132.8 42.6 %collective-permute-start.1 = (bf16[512,256]{1,0:T(8,128)(2,1)S(1)}, bf16[512,256]{1,0:T(8,128)(2,1)S(1)}, u32[]{:S(2)}, u32[]{:S(2)}) collective-permute-start(bf16[512,256]{1,0:T(8,128)(2,1)S(1)} %reduce_sum.18.own_ref), channel_id=1, source_target_pairs={{0,4},{1,5},{2,6},{3,7},{4,8},{5,9},{6,10},{7,11},{8,12},{9,13},{1... | collective-permute-start | bytes 786440 | tf_op jit(solution)/shard_map/ppermute | solution.py:45
  205.6 13.3 %collective-permute-start.3 = (bf16[512,256]{1,0:T(8,128)(2,1)}, bf16[512,256]{1,0:T(8,128)(2,1)S(1)}, u32[]{:S(2)}, u32[]{:S(2)}) collective-permute-start(bf16[512,256]{1,0:T(8,128)(2,1)} %get-tuple-element.18), channel_id=1, source_target_pairs={{8,0},{9,1},{10,2},{11,3},{12,4},{13,5},{14,6},{15,7},{16,8},{17,9... | collective-permute-start | bytes 786440 | tf_op jit(solution)/shard_map/ppermute | solution.py:45
  208.9 10.6 %collective-permute-start.2 = (bf16[512,256]{1,0:T(8,128)(2,1)}, bf16[512,256]{1,0:T(8,128)(2,1)S(1)}, u32[]{:S(2)}, u32[]{:S(2)}) collective-permute-start(bf16[512,256]{1,0:T(8,128)(2,1)} %get-tuple-element.17), channel_id=1, source_target_pairs={{4,0},{5,1},{6,2},{7,3},{8,4},{9,5},{10,6},{11,7},{12,8},{13,9},{1... | collective-permute-start | bytes 786440 | tf_op jit(solution)/shard_map/ppermute | solution.py:45
  219.5 0.7 copy-start.10
  221.3 7.8 %collective-permute-start.4 = (bf16[512,256]{1,0:T(8,128)(2,1)S(1)}, bf16[512,256]{1,0:T(8,128)(2,1)S(1)}, u32[]{:S(2)}, u32[]{:S(2)}) collective-permute-start(bf16[512,256]{1,0:T(8,128)(2,1)S(1)} %get-tuple-element.36), channel_id=1, source_target_pairs={{0,1},{1,0},{2,3},{3,2},{4,5},{5,4},{6,7},{7,6},{8,9},{9,8},{10,11... | collective-permute-start | bytes 786440 | tf_op jit(solution)/shard_map/ppermute | solution.py:54
  244.2 40.2 %collective-permute-start.8 = (bf16[512,512]{0,1:T(8,128)(2,1)}, bf16[512,512]{0,1:T(8,128)(2,1)S(1)}, u32[]{:S(2)}, u32[]{:S(2)}) collective-permute-start(bf16[512,512]{0,1:T(8,128)(2,1)} %bitcast.70), channel_id=1, source_target_pairs={{0,4},{4,8},{8,12},{12,0},{1,5},{5,9},{9,13},{13,1},{2,6},{6,10},{... | collective-permute-start | bytes 1572872 | tf_op jit(solution)/shard_map/ppermute | solution.py:50
  250.5 63.0 %collective-permute-start.9 = (bf16[512,512]{0,1:T(8,128)(2,1)}, bf16[512,512]{0,1:T(8,128)(2,1)S(1)}, u32[]{:S(2)}, u32[]{:S(2)}) collective-permute-start(bf16[512,512]{0,1:T(8,128)(2,1)} %bitcast.71), channel_id=1, source_target_pairs={{0,8},{4,12},{8,0},{12,4},{1,9},{5,13},{9,1},{13,5},{2,10},{6,14},... | collective-permute-start | bytes 1572872 | tf_op jit(solution)/shard_map/ppermute | solution.py:50
  254.3 59.2 %collective-permute-start.10 = (bf16[512,512]{0,1:T(8,128)(2,1)S(1)}, bf16[512,512]{0,1:T(8,128)(2,1)S(1)}, u32[]{:S(2)}, u32[]{:S(2)}) collective-permute-start(bf16[512,512]{0,1:T(8,128)(2,1)S(1)} %bitcast.72), channel_id=1, source_target_pairs={{0,12},{4,0},{8,4},{12,8},{1,13},{5,1},{9,5},{13,9},{2,14},{6,2},{... | collective-permute-start | bytes 1572872 | tf_op jit(solution)/shard_map/ppermute | solution.py:50
  331.9 2.2 copy-start.5
  338.1 2.8 collective-permute-start.11
  342.1 23.5 %all-to-all-start.5 = ((f32[8,32,1024]{2,1,0:T(8,128)}), f32[8,32,1024]{2,1,0:T(8,128)S(1)}, u32[]{:S(2)}, u32[]{:S(2)}) async-start(f32[8,32,1024]{2,1,0:T(8,128)} %bitcast.31), calls=%async_computation.5 | async-start | bytes 2097152 | tf_op jit(solution)/shard_map/all_to_all | solution.py:58
  365.6 27.9 %all-to-all-start.3 = ((bf16[4,2,128,1024]{3,2,1,0:T(8,128)(2,1)}), bf16[4,2,128,1024]{3,2,1,0:T(8,128)(2,1)S(1)}, u32[]{:S(2)}, u32[]{:S(2)}) async-start(bf16[4,2,128,1024]{3,2,1,0:T(8,128)(2,1)} %get-tuple-element.19), calls=%async_computation.3 | async-start | bytes 4194304 | tf_op jit(solution)/shard_map/all_to_all | solution.py:58
  393.5 1.7 copy-start.6
  395.2 35.4 %all-to-all-start.6 = ((f32[8,32,1024]{2,1,0:T(8,128)}), f32[8,32,1024]{2,1,0:T(8,128)S(1)}, u32[]{:S(2)}, u32[]{:S(2)}) async-start(f32[8,32,1024]{2,1,0:T(8,128)} %broadcast_in_dim.17), calls=%async_computation.6 | async-start | bytes 2097152 | tf_op jit(solution)/shard_map/all_to_all | solution.py:58
  399.4 23.8 %collective-permute-start.5 = (bf16[512,256]{1,0:T(8,128)(2,1)S(1)}, bf16[512,256]{1,0:T(8,128)(2,1)S(1)}, u32[]{:S(2)}, u32[]{:S(2)}) collective-permute-start(bf16[512,256]{1,0:T(8,128)(2,1)S(1)} %get-tuple-element.20.d0), channel_id=1, source_target_pairs={{0,1},{1,0},{2,3},{3,2},{4,5},{5,4},{6,7},{7,6},{8,9},{9,8},{10,11... | collective-permute-start | bytes 786440 | tf_op jit(solution)/shard_map/ppermute | solution.py:54
  400.6 22.6 %collective-permute-start.6 = (bf16[512,256]{1,0:T(8,128)(2,1)S(1)}, bf16[512,256]{1,0:T(8,128)(2,1)S(1)}, u32[]{:S(2)}, u32[]{:S(2)}) collective-permute-start(bf16[512,256]{1,0:T(8,128)(2,1)S(1)} %get-tuple-element.20.d0), channel_id=1, source_target_pairs={{0,2},{1,3},{2,0},{3,1},{4,6},{5,7},{6,4},{7,5},{8,10},{9,11},{10,... | collective-permute-start | bytes 786440 | tf_op jit(solution)/shard_map/ppermute | solution.py:54
  401.5 21.7 %collective-permute-start.7 = (bf16[512,256]{1,0:T(8,128)(2,1)S(1)}, bf16[512,256]{1,0:T(8,128)(2,1)S(1)}, u32[]{:S(2)}, u32[]{:S(2)}) collective-permute-start(bf16[512,256]{1,0:T(8,128)(2,1)S(1)} %get-tuple-element.20.d0), channel_id=1, source_target_pairs={{0,3},{1,2},{2,1},{3,0},{4,7},{5,6},{6,5},{7,4},{8,11},{9,10},{10,... | collective-permute-start | bytes 786440 | tf_op jit(solution)/shard_map/ppermute | solution.py:54
  423.2 2.2 copy-start.4
  430.6 6.4 %copy-start.7 = (bf16[4,2,128,1024]{3,2,1,0:T(8,128)(2,1)S(1)}, bf16[4,2,128,1024]{3,2,1,0:T(8,128)(2,1)}, u32[]{:S(2)}) copy-start(bf16[4,2,128,1024]{3,2,1,0:T(8,128)(2,1)} %copy-done.6) | copy-start | bytes 6291460
  430.6 28.9 %all-to-all-start.4 = ((bf16[4,128,2048]{2,1,0:T(8,128)(2,1)}), bf16[4,128,2048]{2,1,0:T(8,128)(2,1)}, u32[]{:S(2)}, u32[]{:S(2)}) async-start(bf16[4,128,2048]{2,1,0:T(8,128)(2,1)} %bitcast.16), calls=%async_computation.4 | async-start | bytes 4194304 | tf_op jit(solution)/shard_map/all_to_all | solution.py:58
  435.2 36.0 %collective-permute-start.12 = (f32[256,1024]{1,0:T(8,128)S(1)}, f32[256,1024]{1,0:T(8,128)}, u32[]{:S(2)}, u32[]{:S(2)}) collective-permute-start(f32[256,1024]{1,0:T(8,128)S(1)} %bitcast.59), channel_id=1, source_target_pairs={{0,16},{16,0},{1,17},{17,1},{2,18},{18,2},{3,19},{19,3},{4,20},{20... | collective-permute-start | bytes 3145736 | tf_op jit(solution)/shard_map/ppermute | solution.py:54
  438.5 3.0 copy-start.8
  466.7 7.7 %copy-start.1 = (f32[4,8]{1,0:T(4,128)S(1)}, f32[4,8]{1,0:T(4,128)}, u32[]{:S(2)}) copy-start(f32[4,8]{1,0:T(4,128)} %param.7) | copy-start | bytes 388
Sparse Core Ops, SparseCore 0:
  11.6 73.8 all-gather.3
  230.2 101.6 all-gather.5

commit v2 on v1

v2 whole, which is shorter than its diff:
```python
import functools

import jax
import jax.numpy as jnp
from jax import lax
from jax.experimental import pallas as pl
from jax.experimental.pallas import tpu as pltpu
from jax.sharding import Mesh
from jax.sharding import PartitionSpec as P

HEADS = 32
KV_HEADS = 4
HEAD = 128
QB = 128
SPAN = 1024
AXES = ("x", "yh", "core", "zh", "zl", "yl")
SIZES = (4, 2, 2, 4, 2, 2)
FSDP = ("zh", "zl", "yl")
GROUP = ("zl", "yl")
PLANE = ("x", "yh")
MEMBERS = 4

FACTOR = 1.0 / float(HEAD) ** 0.5
LOG2E = 1.4426950408889634
NEG = -1e30
F32 = jnp.float32
BF16 = jnp.bfloat16


def nt(a, b):
    return lax.dot_general(a, b, (((1,), (1,)), ((), ())), preferred_element_type=F32)


def nn(a, b):
    return lax.dot_general(a, b, (((1,), (0,)), ((), ())), preferred_element_type=F32)


def tn(a, b):
    return lax.dot_general(a, b, (((0,), (0,)), ((), ())), preferred_element_type=F32)


def shifted(block, axes, distance):
    devices = range(lax.axis_size(axes))
    route = [(i - distance, i) for i in devices if i - distance in devices]
    return lax.ppermute(block, axes, route)


def swapped(block, axes, mask):
    return lax.ppermute(block, axes, [(i, i ^ mask) for i in range(lax.axis_size(axes))])


def fanned(block):
    return [block] + [swapped(block, GROUP, k) for k in range(1, MEMBERS)]


def dealt(blocks):
    return [blocks[0]] + [swapped(blocks[k], GROUP, k) for k in range(1, MEMBERS)]


def exchange(blocks, axes):
    return lax.all_to_all(blocks, axes, split_axis=0, concat_axis=0, tiled=True)


def small(name, grid, in_specs, out_specs, out_shape, kernel, prefetch=0):
    return pl.pallas_call(
        kernel,
        grid_spec=pltpu.PrefetchScalarGridSpec(
            num_scalar_prefetch=prefetch, grid=grid, in_specs=in_specs, out_specs=out_specs
        ),
        out_shape=out_shape,
        compiler_params=pltpu.CompilerParams(vmem_limit_bytes=16 << 20),
        cost_estimate=pl.CostEstimate(flops=0, bytes_accessed=4 << 20, transcendentals=0),
        name=name,
    )


def dequantize_kernel(core_ref, b_ref, s_ref, o_ref):
    del core_ref
    for i in range(b_ref.shape[0] // QB):
        for j in range(b_ref.shape[1] // QB):
            to = (j % KV_HEADS) * 2 + j // KV_HEADS
            block = b_ref[i * QB : (i + 1) * QB, j * QB : (j + 1) * QB].astype(F32)
            scale = s_ref[0, i : i + 1, j : j + 1]
            o_ref[i * QB : (i + 1) * QB, to * QB : (to + 1) * QB] = (block * scale).astype(BF16)


def dequantize(core, blocks, scale):
    rows, cols = blocks.shape
    half = rows // 2
    scale = scale.reshape(2, half // QB, cols // QB)
    return small(
        "dequantize",
        (1,),
        [
            pl.BlockSpec((half, cols), lambda i, c: (c[0], 0)),
            pl.BlockSpec((1,) + scale.shape[1:], lambda i, c: (c[0], 0, 0)),
        ],
        pl.BlockSpec((half, cols), lambda i, c: (0, 0)),
        jax.ShapeDtypeStruct((half, cols), BF16),
        dequantize_kernel,
        1,
    )(core, blocks, scale)


def pack_hidden_kernel(*refs):
    o_ref = refs[-1]
    zhs = len(refs) - 1
    half = refs[0].shape[1] // 2
    for zh, ref in enumerate(refs[:-1]):
        for core in range(2):
            at = (core * zhs + zh) * half
            o_ref[0, :, at : at + half] = ref[:, core * half : (core + 1) * half]


def pack_hidden(hidden, zhs):
    tok, depth = hidden.shape
    quarter = depth // MEMBERS
    piece = quarter // zhs
    return small(
        "pack_hidden",
        (MEMBERS,),
        [pl.BlockSpec((tok, piece), lambda m, z=z: (0, z * MEMBERS + m)) for z in range(zhs)],
        pl.BlockSpec((1, tok, quarter), lambda m: (m, 0, 0)),
        jax.ShapeDtypeStruct((MEMBERS, tok, quarter), hidden.dtype),
        pack_hidden_kernel,
    )(*[hidden] * zhs)


def unpack_hidden_kernel(member_ref, *refs):
    o_ref = refs[-1]
    half = refs[0].shape[1]
    for k in range(MEMBERS):
        for core in range(2):
            at = (2 * (member_ref[0] ^ k) + core) * half
            o_ref[:, pl.ds(pl.multiple_of(at, half), half)] = refs[2 * k + core][...]


def unpack_hidden(member, pieces, zhs):
    tok, quarter = pieces[0].shape
    half = quarter // (2 * zhs)
    specs = [pl.BlockSpec((tok, half), lambda z, m, c=c: (0, c * zhs + z)) for c in range(2)]
    return small(
        "unpack_hidden",
        (zhs,),
        specs * MEMBERS,
        pl.BlockSpec((tok, 2 * half * MEMBERS), lambda z, m: (0, z)),
        jax.ShapeDtypeStruct((tok, quarter * MEMBERS), pieces[0].dtype),
        unpack_hidden_kernel,
        1,
    )(member, *[p for p in pieces for _ in range(2)])


def pack_heads_kernel(q_ref, g_ref, o_ref):
    o_ref[0, 0] = q_ref[...]
    o_ref[0, 1] = g_ref[...]


def pack_heads(queries, grad_out):
    tok, cols = queries.shape
    width = cols // MEMBERS
    block = pl.BlockSpec((tok, width), lambda m: (0, m))
    return small(
        "pack_heads",
        (MEMBERS,),
        [block, block],
        pl.BlockSpec((1, 2, tok, width), lambda m: (m, 0, 0, 0)),
        jax.ShapeDtypeStruct((MEMBERS, 2, tok, width), queries.dtype),
        pack_heads_kernel,
    )(queries, grad_out)


def unpack_heads_kernel(member_ref, *refs):
    a_ref, b_ref = refs[-2:]
    width = refs[0].shape[2]
    for k in range(MEMBERS):
        at = pl.ds(pl.multiple_of((member_ref[0] ^ k) * width, width), width)
        a_ref[:, at] = refs[k][0]
        b_ref[:, at] = refs[k][1]


def unpack_heads(member, pieces):
    _, tok, width = pieces[0].shape
    steps = 4
    rows = tok // steps
    block = pl.BlockSpec((rows, width * MEMBERS), lambda i, m: (i, 0))
    shape = jax.ShapeDtypeStruct((tok, width * MEMBERS), pieces[0].dtype)
    return small(
        "unpack_heads",
        (steps,),
        [pl.BlockSpec((2, rows, width), lambda i, m: (0, i, 0))] * MEMBERS,
        [block, block],
        [shape, shape],
        unpack_heads_kernel,
        1,
    )(member, *pieces)


def turn_kernel(x_ref, o_ref):
    o_ref[...] = x_ref[...].T


def turn(x):
    rows, cols = x.shape
    step = cols // 4
    return small(
        "turn",
        (4,),
        [pl.BlockSpec((rows, step), lambda i: (0, i))],
        pl.BlockSpec((step, rows), lambda i: (i, 0)),
        jax.ShapeDtypeStruct((cols, rows), x.dtype),
        turn_kernel,
    )(x)


def project_kernel(h_ref, w_ref, o_ref):
    o_ref[0] = nn(h_ref[...], w_ref[...])


def project(hidden, weights):
    rows, depth = hidden.shape
    width = weights.shape[1] // MEMBERS
    return pl.pallas_call(
        project_kernel,
        grid=(MEMBERS,),
        in_specs=[
            pl.BlockSpec((rows, depth), lambda h: (0, 0)),
            pl.BlockSpec((depth, width), lambda h: (0, h)),
        ],
        out_specs=pl.BlockSpec((1, rows, width), lambda h: (h, 0, 0)),
        out_shape=jax.ShapeDtypeStruct((MEMBERS, rows, width), F32),
        compiler_params=pltpu.CompilerParams(vmem_limit_bytes=56 << 20),
        cost_estimate=pl.CostEstimate(
            flops=2 * rows * depth * width * MEMBERS, bytes_accessed=8 << 20, transcendentals=0
        ),
        name="project",
    )(hidden, weights)


def attention_kernel(
    place_ref, q_ref, g_ref, far_ref, near_ref, own_ref,
    out_ref, dfar_ref, dnear_ref, down_ref, kv, acc,
):
    t = pl.program_id(0)
    group = own_ref.shape[0]
    tok = q_ref.shape[2]
    pairs = q_ref.shape[3] // (2 * HEAD)
    width = SPAN + tok

    @pl.when(t == 0)
    def _():
        kv[0:group] = far_ref[...]
        kv[group : 2 * group] = near_ref[...]
        kv[2 * group :] = own_ref[...]
        acc[...] = jnp.zeros_like(acc)

    start = pl.multiple_of(t * tok, tok)
    lim = place_ref[t + 1]

    def run(masked):
        keys = kv[pl.ds(start, width), 0:HEAD]
        vals = kv[pl.ds(start, width), HEAD : 2 * HEAD]
        row = lax.broadcasted_iota(jnp.int32, (tok, 2 * tok), 0)
        col = lax.broadcasted_iota(jnp.int32, (tok, 2 * tok), 1) & (tok - 1)
        for pair in range(pairs):
            a = slice(2 * pair * HEAD, (2 * pair + 1) * HEAD)
            b = slice((2 * pair + 1) * HEAD, (2 * pair + 2) * HEAD)
            q2 = jnp.concatenate([q_ref[0, 0, :, a], q_ref[0, 0, :, b]], axis=0)
            g2 = jnp.concatenate([g_ref[0, 0, :, a], g_ref[0, 0, :, b]], axis=0)
            s = nt(keys, q2)
            s = jnp.concatenate(
                [
                    jnp.where(row > col, s[:tok], NEG),
                    s[tok:SPAN],
                    jnp.where(row <= col, s[SPAN:], NEG),
                ],
                axis=0,
            )
            if masked:
                s = jnp.where(lax.broadcasted_iota(jnp.int32, s.shape, 0) >= lim, s, NEG)
            top = jnp.max(s, axis=0, keepdims=True) * (FACTOR * LOG2E)
            expd = jnp.exp2(s * (FACTOR * LOG2E) - top)
            probs = expd * (1.0 / jnp.sum(expd, axis=0, keepdims=True))
            probs_b = probs.astype(BF16)
            dprobs = nt(vals, g2)
            delta = jnp.sum(probs * dprobs, axis=0, keepdims=True)
            dscores = (probs * (dprobs - delta) * FACTOR).astype(BF16)
            acc[pl.ds(start, width), 0:HEAD] += nn(dscores, q2)
            acc[pl.ds(start, width), HEAD : 2 * HEAD] += nn(probs_b, g2)
            output = tn(probs_b, vals).astype(BF16)
            gradq = tn(dscores, keys).astype(BF16)
            out_ref[0, 0, :, a] = output[:tok]
            out_ref[0, 0, :, b] = output[tok:]
            out_ref[0, 1, :, a] = gradq[:tok]
            out_ref[0, 1, :, b] = gradq[tok:]

    @pl.when(lim <= 0)
    def _():
        run(False)

    @pl.when(lim > 0)
    def _():
        run(True)

    @pl.when(t == pl.num_programs(0) - 1)
    def _():
        dfar_ref[...] = acc[0:group].astype(dfar_ref.dtype)
        dnear_ref[...] = acc[group : 2 * group].astype(dnear_ref.dtype)
        down_ref[...] = acc[2 * group :]


def attention(place, queries, far, near, own):
    steps, _, tok, cols = queries.shape
    group, both = own.shape
    whole = pl.BlockSpec((group, both), lambda t, p: (0, 0))
    return pl.pallas_call(
        attention_kernel,
        grid_spec=pltpu.PrefetchScalarGridSpec(
            num_scalar_prefetch=1,
            grid=(steps,),
            in_specs=[
                pl.BlockSpec((1, 1, tok, cols), lambda t, p: (t, 0, 0, 0)),
                pl.BlockSpec((1, 1, tok, cols), lambda t, p: (t, 1, 0, 0)),
                whole,
                whole,
                whole,
            ],
            out_specs=[
                pl.BlockSpec((1, 2, tok, cols), lambda t, p: (t ^ p[0], 0, 0, 0)),
                whole,
                whole,
                whole,
            ],
            scratch_shapes=[
                pltpu.VMEM((3 * group, both), BF16),
                pltpu.VMEM((3 * group, both), F32),
            ],
        ),
        out_shape=[
            jax.ShapeDtypeStruct(queries.shape, BF16),
            jax.ShapeDtypeStruct(own.shape, BF16),
            jax.ShapeDtypeStruct(own.shape, BF16),
            jax.ShapeDtypeStruct(own.shape, F32),
        ],
        compiler_params=pltpu.CompilerParams(vmem_limit_bytes=48 << 20),
        cost_estimate=pl.CostEstimate(
            flops=30_000_000_000, bytes_accessed=6 << 20, transcendentals=5_000_000
        ),
        name="attention",
    )(place, queries, queries, far, near, own)


def grad_hidden_kernel(member_ref, d0, d1, d2, d3, w_ref, o_ref):
    total = None
    for k, d in enumerate((d0, d1, d2, d3)):
        width = d.shape[1]
        at = pl.multiple_of((member_ref[0] ^ k) * width, width)
        term = nt(d[...], w_ref[:, pl.ds(at, width)])
        total = term if total is None else total + term
    tok = o_ref.shape[1]
    for t in range(MEMBERS):
        o_ref[member_ref[0] ^ t] = total[t * tok : (t + 1) * tok].astype(BF16)


def grad_hidden_quarter(member, pieces, weights):
    rows, width = pieces[0].shape
    depth, cols = weights.shape
    step = 256
    piece = pl.BlockSpec((rows, width), lambda i, m: (0, 0))
    return pl.pallas_call(
        grad_hidden_kernel,
        grid_spec=pltpu.PrefetchScalarGridSpec(
            num_scalar_prefetch=1,
            grid=(depth // step,),
            in_specs=[piece] * 4 + [pl.BlockSpec((step, cols), lambda i, m: (i, 0))],
            out_specs=pl.BlockSpec((MEMBERS, rows // MEMBERS, step), lambda i, m: (0, 0, i)),
        ),
        out_shape=jax.ShapeDtypeStruct((MEMBERS, rows // MEMBERS, depth), BF16),
        compiler_params=pltpu.CompilerParams(vmem_limit_bytes=32 << 20),
        cost_estimate=pl.CostEstimate(
            flops=2 * rows * depth * cols, bytes_accessed=8 << 20, transcendentals=0
        ),
        name="grad_hidden",
    )(member, *pieces, weights)


def weight_grad_kernel(member_ref, h_ref, d0, d1, d2, d3, theirs_ref, mine_ref, *, steps):
    def run(o_ref):
        planes, _, rows, cols = o_ref.shape
        for k, d in enumerate((d0, d1, d2, d3)):
            at = pl.multiple_of((member_ref[0] ^ k) * HEAD, HEAD)
            term = nn(h_ref[...], d[...]).astype(o_ref.dtype).reshape(planes, rows, 2 * HEAD)
            o_ref[:, 0, :, pl.ds(at, HEAD)] = term[:, :, :HEAD]
            o_ref[:, 0, :, pl.ds(cols // 2 + at, HEAD)] = term[:, :, HEAD:]

    @pl.when(pl.program_id(0) < steps)
    def _():
        run(theirs_ref)

    @pl.when(pl.program_id(0) >= steps)
    def _():
        run(mine_ref)


def weight_grad_share(place, turned, pieces, steps, planes):
    feats, tokens = turned.shape
    both = pieces[0].shape[1]
    cols = both * KV_HEADS
    step = feats // (2 * steps)
    rows = step // planes

    def block(i, p):
        return (jnp.where(p[1] == 0, (i + steps) % (2 * steps), i), 0)

    piece = pl.BlockSpec((tokens, both), lambda i, p: (0, 0))
    out = (planes, 1, rows, cols)
    return pl.pallas_call(
        functools.partial(weight_grad_kernel, steps=steps),
        grid_spec=pltpu.PrefetchScalarGridSpec(
            num_scalar_prefetch=1,
            grid=(2 * steps,),
            in_specs=[pl.BlockSpec((step, tokens), block)] + [piece] * 4,
            out_specs=[
                pl.BlockSpec(out, lambda i, p: (0, jnp.minimum(i, steps - 1), 0, 0)),
                pl.BlockSpec(out, lambda i, p: (0, jnp.maximum(i - steps, 0), 0, 0)),
            ],
        ),
        out_shape=[
            jax.ShapeDtypeStruct((planes, steps, rows, cols), BF16),
            jax.ShapeDtypeStruct((planes, steps, rows, cols), F32),
        ],
        compiler_params=pltpu.CompilerParams(vmem_limit_bytes=32 << 20),
        cost_estimate=pl.CostEstimate(
            flops=2 * feats * tokens * cols, bytes_accessed=10 << 20, transcendentals=0
        ),
        name="weight_grad",
    )(place, turned, *pieces)


def body(hidden, kv_blocks, kv_scale, queries, grad_out):
    tok = hidden.shape[0]
    half = kv_blocks.shape[0] // 2
    kv_cols = kv_blocks.shape[1]
    zh = lax.axis_index("zh")
    core = lax.axis_index("core").reshape(1)
    member = lax.axis_index(GROUP).reshape(1)
    zhs = lax.axis_size("zh")
    planes = lax.axis_size(PLANE)

    rows = dequantize(core, kv_blocks, kv_scale)
    weights = lax.all_gather(rows, ("core", "zh"), axis=0, tiled=True)
    quarter = exchange(pack_hidden(hidden, zhs), GROUP).reshape(MEMBERS * tok, -1)
    heads = exchange(pack_heads(queries, grad_out), GROUP)

    weights, quarter, heads = lax.optimization_barrier((weights, quarter, heads))
    partial = exchange(project(quarter, weights), GROUP)
    own = jnp.sum(partial, axis=0).astype(BF16)
    far = shifted(own, AXES, 2 * MEMBERS)
    near = shifted(own, AXES, MEMBERS)
    quarter, own = lax.optimization_barrier((quarter, own))
    turned = turn(quarter)

    first = lax.axis_index(AXES) // MEMBERS * MEMBERS
    lim = jnp.maximum(0, SPAN - (first + jnp.arange(MEMBERS, dtype=jnp.int32)) * tok)
    far, near, turned = lax.optimization_barrier((far, near, turned))
    out, dfar, dnear, down = attention(
        jnp.concatenate([member, lim]).astype(jnp.int32), heads, far, near, own
    )
    from_far = shifted(dfar, AXES, -2 * MEMBERS).astype(F32)
    from_near = shifted(dnear, AXES, -MEMBERS).astype(F32)
    all_grad = (down + from_near + from_far).astype(BF16)
    inside = down + jnp.where(zh + 1 < zhs, from_near, 0.0) + jnp.where(zh + 2 < zhs, from_far, 0.0)
    seg_grad = inside.astype(BF16)

    alls = fanned(all_grad)
    place = jnp.concatenate([member, core]).astype(jnp.int32)
    theirs, mine = weight_grad_share(place, turned, alls, zhs, planes)

    out, seg_grad, theirs = lax.optimization_barrier((out, seg_grad, theirs))
    outs = dealt(out)
    segs = fanned(seg_grad)
    mine = (mine + swapped(theirs, "core", 1).astype(F32)).astype(BF16)
    mine, segs = lax.optimization_barrier((mine, segs))
    back = grad_hidden_quarter(member, segs, weights)
    parts = exchange(mine, PLANE)
    parts, outs, back = lax.optimization_barrier((parts, outs, back))
    backs = dealt(back)
    parts = jnp.sum(parts.astype(F32), axis=0)
    summed = jnp.sum(exchange(parts, "zh"), axis=0)
    spread = exchange(jnp.broadcast_to(summed[None], (planes,) + summed.shape), PLANE)
    backs, spread = lax.optimization_barrier((backs, spread))
    spread = spread.reshape(half, kv_cols)
    opposite = swapped(spread, "core", 1)
    attn_out, grad_queries = unpack_heads(member, outs)
    grad_hidden = unpack_hidden(member, backs, zhs)
    weight_grad = jnp.where(
        core[0] == 0,
        jnp.concatenate([spread, opposite], axis=0),
        jnp.concatenate([opposite, spread], axis=0),
    )
    return (attn_out, grad_queries, grad_hidden, weight_grad)


def solution(mesh):
    finer = Mesh(mesh.devices.reshape(SIZES), AXES)
    placed = (P(AXES, None), P(FSDP, None), P(FSDP, None), P(AXES, None), P(AXES, None))
    return jax.shard_map(
        body,
        mesh=finer,
        in_specs=placed,
        out_specs=(P(AXES, None), P(AXES, None), P(AXES, None), P(FSDP, None)),
        check_vma=False,
    )
```

time: 484 us -> 393 us (0.81)
  waiting for transfers between devices: 225 us -> 157 us
  local copies, waits for them, and re-layouts: 65.3 us -> 18.2 us
  starting transfers between devices: 60.7 us -> 73.5 us
  Pallas kernels: 42.8 us -> 52.1 us
    ppermute x3 -> x0, waiting for transfers between devices: 54.7 us -> none  [rotated(): lax.ppermute(block, axis, [(i, (i + distance) % size) for i in range(size)])]
    ppermute x6 -> x14, waiting for transfers between devices: 29.5 us -> 80.4 us  [swapped(): lax.ppermute(block, axes, [(i, i ^ mask) for i in range(lax.axis_size(axe...]
    all_to_all x6 -> x3, waiting for transfers between devices: 71.9 us -> 44.1 us  [exchange(): return lax.all_to_all(blocks, axes, split_axis=0, concat_axis=0, tiled=True)]
    reshape x10 -> x0, local copies, waits for them, and re-layouts: 21.8 us -> none  [the longest x3 11.6 us: body(): back.reshape(MEMBERS, tok, 2, zhs, half).transpose(1, 3, 0, 2, 4)]
    all_gather x1 -> x0, waiting for transfers between devices: 18.4 us -> none  [body(): gathered = lax.all_gather(pair, ('zh', 'zl'), axis=0, tiled=True)]
    ppermute x6 -> x14, starting transfers between devices: 6.76 us -> 22 us  [swapped(): lax.ppermute(block, axes, [(i, i ^ mask) for i in range(lax.axis_size(axe...]
    ppermute x4, waiting for transfers between devices: 45 us -> 32.9 us  [shifted(): return lax.ppermute(block, axes, route)]
    ppermute x4, starting transfers between devices: 16.2 us -> 25.6 us  [shifted(): return lax.ppermute(block, axes, route)]
  transfers between devices with their start and end apart: 21 -> 22, of which waited for: 15 -> 14; matrix products, arithmetic and copies ran while one was open for 11% -> 1% of each run, Pallas kernels for 1% -> 3%
where the time goes in v2:
time: 393 us; the launch traced here: 390 us
  waiting for transfers between devices  157 us (40%)
  starting transfers between devices  73.5 us (19%)
  blocking collectives  63.3 us (16%)
  Pallas kernels  52.1 us (13%)
  local copies, waits for them, and re-layouts  18.2 us (5%)
  between operations  14.3 us (4%)
  other arithmetic  11.5 us (3%)
    ppermute x14, waiting for transfers between devices, swapped(): lax.ppermute(block, axes, [(i, i ^ mask) for i in range(lax.axis_size(axe...  80.4 us
    all_to_all x3, blocking collectives, exchange(): return lax.all_to_all(blocks, axes, split_axis=0, concat_axis=0, tiled=True)  63.3 us
    all_to_all x3, waiting for transfers between devices, exchange(): return lax.all_to_all(blocks, axes, split_axis=0, concat_axis=0, tiled=True)  44.1 us
    ppermute x4, waiting for transfers between devices, shifted(): return lax.ppermute(block, axes, route)  32.9 us
    pallas_call x1, Pallas kernels, attention(): pl.pallas_call(attention_kernel, grid_spec=pltpu.PrefetchScalarGridSpec(n...  29 us
    all_to_all x3, starting transfers between devices, exchange(): return lax.all_to_all(blocks, axes, split_axis=0, concat_axis=0, tiled=True)  25.9 us
    ppermute x4, starting transfers between devices, shifted(): return lax.ppermute(block, axes, route)  25.6 us
    ppermute x14, starting transfers between devices, swapped(): lax.ppermute(block, axes, [(i, i ^ mask) for i in range(lax.axis_size(axe...  22 us
  transfers between devices with their start and end apart: 22, of which 14 were waited for; matrix products, arithmetic and copies ran while one was open for 1% of the time, Pallas kernels for 3%

profile of v2, /device:TPU:1, one launch (start us, length us, event | category | flops | bytes accessed | tf_op | source)
XLA Modules:
  0.0 390.3 jit_solution(9651160348605735660)
XLA Ops:
  12.2 4.9 %all-to-all-start = ((bf16[4,128,2048]{2,1,0:T(8,128)(2,1)}), bf16[4,128,2048]{2,1,0:T(8,128)(2,1)S(1)}, u32[]{:S(2)}, u32[]{:S(2)}) async-start(bf16[4,128,2048]{2,1,0:T(8,128)(2,1)} %copy-done.3), calls=%async_computation | async-start | bytes 4194304 | tf_op jit(solution)/shard_map/all_to_all | solution.py:61
  20.0 44.1 %all-to-all-done = bf16[4,128,2048]{2,1,0:T(8,128)(2,1)S(1)} async-done(((bf16[4,128,2048]{2,1,0:T(8,128)(2,1)}), bf16[4,128,2048]{2,1,0:T(8,128)(2,1)S(1)}, u32[]{:S(2)}, u32[]{:S(2)}) %all-to-all-start) | async-done | bytes 2097184 | tf_op jit(solution)/shard_map/all_to_all | solution.py:61
  64.1 27.3 %all_to_all.30.q_ref.g_ref = bf16[4,2,128,1024]{3,2,1,0:T(8,128)(2,1)} all-to-all(bf16[4,2,128,1024]{3,2,1,0:T(8,128)(2,1)} %copy-done.4), channel_id=1, replica_groups=mesh['x'=4,'yh'=2,'core'=2,'zh'=4,'zl'=2,'yl'=2] {'zl','yl'}, dimensions={0} | all-to-all | bytes 4194304 | tf_op jit(solution)/shard_map/all_to_all | solution.py:61
  91.4 6.4 %project.1 = f32[4,512,256]{2,1,0:T(8,128)} custom-call(bf16[512,2048]{1,0:T(8,128)(2,1)} %bitcast.21, bf16[2048,1024]{1,0:T(8,128)(2,1)} %all-gather.2.cloned.1.call-done.w_ref), custom_call_target="tpu_custom_call" | custom-call | flops 2147483648 | bytes 8388608 | tf_op jit(solution)/shard_map/project/pallas_call | solution.py:222
  97.8 21.0 %all_to_all.31 = f32[4,512,256]{2,1,0:T(8,128)} all-to-all(f32[4,512,256]{2,1,0:T(8,128)} %project.1), channel_id=1, replica_groups=mesh['x'=4,'yh'=2,'core'=2,'zh'=4,'zl'=2,'yl'=2] {'zl','yl'}, dimensions={0} | all-to-all | bytes 4194304 | tf_op jit(solution)/shard_map/all_to_all | solution.py:61
  120.7 9.9 %collective-permute-start.1 = (bf16[512,256]{1,0:T(8,128)(2,1)S(1)}, bf16[512,256]{1,0:T(8,128)(2,1)S(1)}, u32[]{:S(2)}, u32[]{:S(2)}) collective-permute-start(bf16[512,256]{1,0:T(8,128)(2,1)S(1)} %reduce_sum.27.own_ref), channel_id=1, source_target_pairs={{0,4},{1,5},{2,6},{3,7},{4,8},{5,9},{6,10},{7,11},{8,12},{9,13},{1... | collective-permute-start | bytes 786440 | tf_op jit(solution)/shard_map/ppermute | solution.py:45
  130.6 11.8 %collective-permute-start = (bf16[512,256]{1,0:T(8,128)(2,1)S(1)}, bf16[512,256]{1,0:T(8,128)(2,1)S(1)}, u32[]{:S(2)}, u32[]{:S(2)}) collective-permute-start(bf16[512,256]{1,0:T(8,128)(2,1)S(1)} %reduce_sum.27.own_ref), channel_id=1, source_target_pairs={{0,8},{1,9},{2,10},{3,11},{4,12},{5,13},{6,14},{7,15},{8,16},{9,17... | collective-permute-start | bytes 786440 | tf_op jit(solution)/shard_map/ppermute | solution.py:45
  143.5 8.3 %collective-permute-done.1.near_ref = bf16[512,256]{1,0:T(8,128)(2,1)S(1)} collective-permute-done((bf16[512,256]{1,0:T(8,128)(2,1)S(1)}, bf16[512,256]{1,0:T(8,128)(2,1)S(1)}, u32[]{:S(2)}, u32[]{:S(2)}) %collective-permute-start.1) | collective-permute-done | bytes 262176 | tf_op jit(solution)/shard_map/ppermute | solution.py:45
  151.9 12.4 %collective-permute-done.far_ref = bf16[512,256]{1,0:T(8,128)(2,1)S(1)} collective-permute-done((bf16[512,256]{1,0:T(8,128)(2,1)S(1)}, bf16[512,256]{1,0:T(8,128)(2,1)S(1)}, u32[]{:S(2)}, u32[]{:S(2)}) %collective-permute-start) | collective-permute-done | bytes 262176 | tf_op jit(solution)/shard_map/ppermute | solution.py:45
  164.3 29.0 %attention.1 = (bf16[4,2,128,1024]{3,2,1,0:T(8,128)(2,1)S(1)}, bf16[512,256]{1,0:T(8,128)(2,1)}, bf16[512,256]{1,0:T(8,128)(2,1)}, f32[512,256]{1,0:T(8,128)S(1)}) custom-call(s32[5]{0:T(128)S(1)} %pad_add_fusion.1.place_ref, bf16[4,2,128,1024]{3,2,1,0:T(8,128)(2,1)S(1)} %copy-done.6, bf16[4,2,128,1024]{3,2,1,0:T(8,128)(2,1)S(1)} %copy-done.6, ...), custom_call_target="tpu_custom_call" | custom-call | flops 30000001024 | bytes 6291456 | tf_op jit(solution)/shard_map/attention/pallas_call | solution.py:315
  197.2 12.1 %collective-permute-done.2 = bf16[512,256]{1,0:T(8,128)(2,1)S(1)} collective-permute-done((bf16[512,256]{1,0:T(8,128)(2,1)}, bf16[512,256]{1,0:T(8,128)(2,1)S(1)}, u32[]{:S(2)}, u32[]{:S(2)}) %collective-permute-start.2) | collective-permute-done | bytes 262176 | tf_op jit(solution)/shard_map/ppermute | solution.py:45
  209.5 5.8 %collective-permute-start.6 = (bf16[512,256]{1,0:T(8,128)(2,1)S(1)}, bf16[512,256]{1,0:T(8,128)(2,1)S(1)}, u32[]{:S(2)}, u32[]{:S(2)}) collective-permute-start(bf16[512,256]{1,0:T(8,128)(2,1)S(1)} %get-tuple-element.83.d0), channel_id=1, source_target_pairs={{0,3},{1,2},{2,1},{3,0},{4,7},{5,6},{6,5},{7,4},{8,11},{9,10},{10,... | collective-permute-start | bytes 786440 | tf_op jit(solution)/shard_map/ppermute | solution.py:49
  216.9 3.9 %collective-permute-done.6.d3 = bf16[512,256]{1,0:T(8,128)(2,1)S(1)} collective-permute-done((bf16[512,256]{1,0:T(8,128)(2,1)S(1)}, bf16[512,256]{1,0:T(8,128)(2,1)S(1)}, u32[]{:S(2)}, u32[]{:S(2)}) %collective-permute-start.6) | collective-permute-done | bytes 262176 | tf_op jit(solution)/shard_map/ppermute | solution.py:49
  220.9 4.6 %collective-permute-done.5.d2 = bf16[512,256]{1,0:T(8,128)(2,1)S(1)} collective-permute-done((bf16[512,256]{1,0:T(8,128)(2,1)S(1)}, bf16[512,256]{1,0:T(8,128)(2,1)S(1)}, u32[]{:S(2)}, u32[]{:S(2)}) %collective-permute-start.5) | collective-permute-done | bytes 262176 | tf_op jit(solution)/shard_map/ppermute | solution.py:49
  227.1 5.5 %weight_grad.1 = (bf16[8,4,32,1024]{3,2,1,0:T(8,128)(2,1)S(1)}, f32[8,4,32,1024]{3,2,1,0:T(8,128)S(1)}) custom-call(s32[2]{0:T(128)S(1)} %pad_add_fusion.member_ref, bf16[2048,512]{1,0:T(8,128)(2,1)S(1)} %copy-done.8, bf16[512,256]{1,0:T(8,128)(2,1)S(1)} %get-tuple-element.83.d0, bf16[512,256]{1,0:T(8,128)(2,1)S(1)} %collective-permute-done.4.d1, ...), custom_call_target="tpu_custom_call" | custom-call | flops 2147483648 | bytes 10485760 | tf_op jit(solution)/shard_map/weight_grad/pallas_call | solution.py:416
  232.7 2.8 collective-permute-start.10
  237.1 2.1 add_convert_fusion
  239.2 2.6 collective-permute-done.10.d3
  241.8 6.3 %collective-permute-done.9.d2 = bf16[512,256]{1,0:T(8,128)(2,1)S(1)} collective-permute-done((bf16[512,256]{1,0:T(8,128)(2,1)S(1)}, bf16[512,256]{1,0:T(8,128)(2,1)S(1)}, u32[]{:S(2)}, u32[]{:S(2)}) %collective-permute-start.9) | collective-permute-done | bytes 262176 | tf_op jit(solution)/shard_map/ppermute | solution.py:49
  248.9 11.2 %all-to-all-start.3 = ((bf16[8,4,32,1024]{3,2,1,0:T(8,128)(2,1)}), bf16[8,4,32,1024]{3,2,1,0:T(8,128)(2,1)}, u32[]{:S(2)}, u32[]{:S(2)}) async-start(bf16[8,4,32,1024]{3,2,1,0:T(8,128)(2,1)} %add_convert_fusion), calls=%async_computation.3 | async-start | bytes 4194304 | tf_op jit(solution)/shard_map/all_to_all | solution.py:61
  266.7 4.2 %grad_hidden.1 = bf16[4,128,2048]{2,1,0:T(8,128)(2,1)S(1)} custom-call(s32[1]{0:T(128)} %bitcast.member_ref, bf16[512,256]{1,0:T(8,128)(2,1)S(1)} %get-tuple-element.57.d0, bf16[512,256]{1,0:T(8,128)(2,1)S(1)} %copy-done.24, bf16[512,256]{1,0:T(8,128)(2,1)S(1)} %copy-done.22, bf16[512,256]{1,0:T(8,128)(2,1)S(1)} %copy-done.20, bf16[2048,1024]{1,0:T(8,128)(2,1)S(1)} %copy-done.5), custom_call_target="tpu_custom_call" | custom-call | flops 2147483648 | bytes 8388608 | tf_op jit(solution)/shard_map/grad_hidden/pallas_call | solution.py:369
  270.9 14.8 %collective-permute-done.13.refs_3_ = bf16[2,128,1024]{2,1,0:T(8,128)(2,1)S(1)} collective-permute-done((bf16[2,128,1024]{2,1,0:T(8,128)(2,1)S(1)}, bf16[2,128,1024]{2,1,0:T(8,128)(2,1)S(1)}, u32[]{:S(2)}, u32[]{:S(2)}) %collective-permute-start.13) | collective-permute-done | bytes 524320 | tf_op jit(solution)/shard_map/ppermute | solution.py:49
  286.5 10.4 %collective-permute-done.12.refs_2_ = bf16[2,128,1024]{2,1,0:T(8,128)(2,1)S(1)} collective-permute-done((bf16[2,128,1024]{2,1,0:T(8,128)(2,1)S(1)}, bf16[2,128,1024]{2,1,0:T(8,128)(2,1)S(1)}, u32[]{:S(2)}, u32[]{:S(2)}) %collective-permute-start.12) | collective-permute-done | bytes 524320 | tf_op jit(solution)/shard_map/ppermute | solution.py:49
  297.7 8.5 %collective-permute-done.11.refs_1_ = bf16[2,128,1024]{2,1,0:T(8,128)(2,1)S(1)} collective-permute-done((bf16[2,128,1024]{2,1,0:T(8,128)(2,1)S(1)}, bf16[2,128,1024]{2,1,0:T(8,128)(2,1)S(1)}, u32[]{:S(2)}, u32[]{:S(2)}) %collective-permute-start.11) | collective-permute-done | bytes 524320 | tf_op jit(solution)/shard_map/ppermute | solution.py:49
  306.9 2.0 convert_reduce_fusion
  308.9 15.1 %all_to_all.32 = f32[4,32,1024]{2,1,0:T(8,128)} all-to-all(f32[4,32,1024]{2,1,0:T(8,128)S(1)} %convert_reduce_fusion), channel_id=1, replica_groups=mesh['x'=4,'yh'=2,'core'=2,'zh'=4,'zl'=2,'yl'=2] {'zh'}, dimensions={0} | all-to-all | bytes 1048576 | tf_op jit(solution)/shard_map/all_to_all | solution.py:61
  326.2 9.8 %all-to-all-start.5 = ((f32[8,32,1024]{2,1,0:T(8,128)}), f32[8,32,1024]{2,1,0:T(8,128)}, u32[]{:S(2)}, u32[]{:S(2)}) async-start(f32[8,32,1024]{2,1,0:T(8,128)} %broadcast_in_dim.12), calls=%async_computation.5 | async-start | bytes 2097152 | tf_op jit(solution)/shard_map/all_to_all | solution.py:61
  336.2 4.0 %collective-permute-start.16 = (bf16[128,2048]{1,0:T(8,128)(2,1)S(1)}, bf16[128,2048]{1,0:T(8,128)(2,1)S(1)}, u32[]{:S(2)}, u32[]{:S(2)}) collective-permute-start(bf16[128,2048]{1,0:T(8,128)(2,1)S(1)} %get-tuple-element.74), channel_id=1, source_target_pairs={{0,3},{1,2},{2,1},{3,0},{4,7},{5,6},{6,5},{7,4},{8,11},{9,10},{10,... | collective-permute-start | bytes 1572872 | tf_op jit(solution)/shard_map/ppermute | solution.py:49
  341.1 17.3 %collective-permute-done.16.refs_6_.refs_7_ = bf16[128,2048]{1,0:T(8,128)(2,1)S(1)} collective-permute-done((bf16[128,2048]{1,0:T(8,128)(2,1)S(1)}, bf16[128,2048]{1,0:T(8,128)(2,1)S(1)}, u32[]{:S(2)}, u32[]{:S(2)}) %collective-permute-start.16) | collective-permute-done | bytes 524320 | tf_op jit(solution)/shard_map/ppermute | solution.py:49
  358.4 11.2 %collective-permute-done.15.refs_4_.refs_5_ = bf16[128,2048]{1,0:T(8,128)(2,1)S(1)} collective-permute-done((bf16[128,2048]{1,0:T(8,128)(2,1)S(1)}, bf16[128,2048]{1,0:T(8,128)(2,1)S(1)}, u32[]{:S(2)}, u32[]{:S(2)}) %collective-permute-start.15) | collective-permute-done | bytes 524320 | tf_op jit(solution)/shard_map/ppermute | solution.py:49
  377.2 2.2 unpack_hidden.1
  379.4 4.1 %maximum_select_fusion = f32[512,1024]{1,0:T(8,128)} fusion(f32[256,1024]{1,0:T(8,128)} %collective-permute-done.17, f32[256,1024]{1,0:T(8,128)} %bitcast.12, pred[]{:T(512)S(6)} %eq.3), kind=kLoop, calls=%fused_computation.2 | loop fusion | flops 1572864 | bytes 4194305 | tf_op jit(solution)/shard_map/jit(_where)/select_n | solution.py:495
  (88 shorter events, 40.4 us)
Async XLA Ops:
  7.2 3.2 copy-start
  7.2 84.2 %all-gather.2.cloned.1.call-start = ((), (), s32[]{:S(2)}) async-start(), calls=%async_computation.6 | async-start | bytes 4718592 | tf_op jit(solution)/shard_map/all_gather | solution.py:450
  7.2 1.4 copy-start.9
  12.2 4.9 %copy-start.10 = (bf16[128,4096]{1,0:T(8,128)(2,1)S(1)}, bf16[128,4096]{1,0:T(8,128)(2,1)}, u32[]{:S(2)}) copy-start(bf16[128,4096]{1,0:T(8,128)(2,1)} %q_ref.1) | copy-start | bytes 3145732
  12.2 51.9 %all-to-all-start = ((bf16[4,128,2048]{2,1,0:T(8,128)(2,1)}), bf16[4,128,2048]{2,1,0:T(8,128)(2,1)S(1)}, u32[]{:S(2)}, u32[]{:S(2)}) async-start(bf16[4,128,2048]{2,1,0:T(8,128)(2,1)} %copy-done.3), calls=%async_computation | async-start | bytes 4194304 | tf_op jit(solution)/shard_map/all_to_all | solution.py:61
  64.1 27.3 %copy-start.1 = (bf16[4,128,2048]{2,1,0:T(8,128)(2,1)}, bf16[4,128,2048]{2,1,0:T(8,128)(2,1)S(1)}, u32[]{:S(2)}) copy-start(bf16[4,128,2048]{2,1,0:T(8,128)(2,1)S(1)} %all-to-all-done) | copy-start | bytes 6291460
  118.8 23.8 %copy-start.2 = (bf16[4,128,2048]{2,1,0:T(8,128)(2,1)S(1)}, bf16[4,128,2048]{2,1,0:T(8,128)(2,1)}, u32[]{:S(2)}) copy-start(bf16[4,128,2048]{2,1,0:T(8,128)(2,1)} %copy-done.1) | copy-start | bytes 6291460
  120.7 31.2 %collective-permute-start.1 = (bf16[512,256]{1,0:T(8,128)(2,1)S(1)}, bf16[512,256]{1,0:T(8,128)(2,1)S(1)}, u32[]{:S(2)}, u32[]{:S(2)}) collective-permute-start(bf16[512,256]{1,0:T(8,128)(2,1)S(1)} %reduce_sum.27.own_ref), channel_id=1, source_target_pairs={{0,4},{1,5},{2,6},{3,7},{4,8},{5,9},{6,10},{7,11},{8,12},{9,13},{1... | collective-permute-start | bytes 786440 | tf_op jit(solution)/shard_map/ppermute | solution.py:45
  130.6 33.7 %collective-permute-start = (bf16[512,256]{1,0:T(8,128)(2,1)S(1)}, bf16[512,256]{1,0:T(8,128)(2,1)S(1)}, u32[]{:S(2)}, u32[]{:S(2)}) collective-permute-start(bf16[512,256]{1,0:T(8,128)(2,1)S(1)} %reduce_sum.27.own_ref), channel_id=1, source_target_pairs={{0,8},{1,9},{2,10},{3,11},{4,12},{5,13},{6,14},{7,15},{8,16},{9,17... | collective-permute-start | bytes 786440 | tf_op jit(solution)/shard_map/ppermute | solution.py:45
  142.6 21.7 %copy-start.6 = (bf16[4,2,128,1024]{3,2,1,0:T(8,128)(2,1)S(1)}, bf16[4,2,128,1024]{3,2,1,0:T(8,128)(2,1)}, u32[]{:S(2)}) copy-start(bf16[4,2,128,1024]{3,2,1,0:T(8,128)(2,1)} %all_to_all.30.q_ref.g_ref) | copy-start | bytes 6291460
  143.5 49.8 %copy-start.7 = (bf16[2048,512]{1,0:T(8,128)(2,1)}, bf16[2048,512]{1,0:T(8,128)(2,1)S(1)}, u32[]{:S(2)}) copy-start(bf16[2048,512]{1,0:T(8,128)(2,1)S(1)} %turn.1.h_ref) | copy-start | bytes 6291460
  193.3 16.0 %collective-permute-start.2 = (bf16[512,256]{1,0:T(8,128)(2,1)}, bf16[512,256]{1,0:T(8,128)(2,1)S(1)}, u32[]{:S(2)}, u32[]{:S(2)}) collective-permute-start(bf16[512,256]{1,0:T(8,128)(2,1)} %get-tuple-element.48), channel_id=1, source_target_pairs={{4,0},{5,1},{6,2},{7,3},{8,4},{9,5},{10,6},{11,7},{12,8},{13,9},{1... | collective-permute-start | bytes 786440 | tf_op jit(solution)/shard_map/ppermute | solution.py:45
  195.2 14.1 %collective-permute-start.3 = (bf16[512,256]{1,0:T(8,128)(2,1)}, bf16[512,256]{1,0:T(8,128)(2,1)S(1)}, u32[]{:S(2)}, u32[]{:S(2)}) collective-permute-start(bf16[512,256]{1,0:T(8,128)(2,1)} %get-tuple-element.49), channel_id=1, source_target_pairs={{8,0},{9,1},{10,2},{11,3},{12,4},{13,5},{14,6},{15,7},{16,8},{17,9... | collective-permute-start | bytes 786440 | tf_op jit(solution)/shard_map/ppermute | solution.py:45
  209.5 11.4 %collective-permute-start.6 = (bf16[512,256]{1,0:T(8,128)(2,1)S(1)}, bf16[512,256]{1,0:T(8,128)(2,1)S(1)}, u32[]{:S(2)}, u32[]{:S(2)}) collective-permute-start(bf16[512,256]{1,0:T(8,128)(2,1)S(1)} %get-tuple-element.83.d0), channel_id=1, source_target_pairs={{0,3},{1,2},{2,1},{3,0},{4,7},{5,6},{6,5},{7,4},{8,11},{9,10},{10,... | collective-permute-start | bytes 786440 | tf_op jit(solution)/shard_map/ppermute | solution.py:49
  215.3 10.2 %collective-permute-start.5 = (bf16[512,256]{1,0:T(8,128)(2,1)S(1)}, bf16[512,256]{1,0:T(8,128)(2,1)S(1)}, u32[]{:S(2)}, u32[]{:S(2)}) collective-permute-start(bf16[512,256]{1,0:T(8,128)(2,1)S(1)} %get-tuple-element.83.d0), channel_id=1, source_target_pairs={{0,2},{1,3},{2,0},{3,1},{4,6},{5,7},{6,4},{7,5},{8,10},{9,11},{10,... | collective-permute-start | bytes 786440 | tf_op jit(solution)/shard_map/ppermute | solution.py:49
  215.8 9.8 %collective-permute-start.4 = (bf16[512,256]{1,0:T(8,128)(2,1)S(1)}, bf16[512,256]{1,0:T(8,128)(2,1)S(1)}, u32[]{:S(2)}, u32[]{:S(2)}) collective-permute-start(bf16[512,256]{1,0:T(8,128)(2,1)S(1)} %get-tuple-element.83.d0), channel_id=1, source_target_pairs={{0,1},{1,0},{2,3},{3,2},{4,5},{5,4},{6,7},{7,6},{8,9},{9,8},{10,11... | collective-permute-start | bytes 786440 | tf_op jit(solution)/shard_map/ppermute | solution.py:49
  225.5 1.6 copy-start.8
  232.6 4.5 %collective-permute-start.7 = (bf16[8,4,32,1024]{3,2,1,0:T(8,128)(2,1)S(1)}, bf16[8,4,32,1024]{3,2,1,0:T(8,128)(2,1)S(1)}, u32[]{:S(2)}, u32[]{:S(2)}) collective-permute-start(bf16[8,4,32,1024]{3,2,1,0:T(8,128)(2,1)S(1)} %get-tuple-element.53), channel_id=1, source_target_pairs={{0,16},{16,0},{1,17},{17,1},{2,18},{18,2},{3,19},{19,3},{4,20},{20... | collective-permute-start | bytes 6291464 | tf_op jit(solution)/shard_map/ppermute | solution.py:49
  232.7 9.1 %collective-permute-start.10 = (bf16[512,256]{1,0:T(8,128)(2,1)S(1)}, bf16[512,256]{1,0:T(8,128)(2,1)S(1)}, u32[]{:S(2)}, u32[]{:S(2)}) collective-permute-start(bf16[512,256]{1,0:T(8,128)(2,1)S(1)} %get-tuple-element.57.d0), channel_id=1, source_target_pairs={{0,3},{1,2},{2,1},{3,0},{4,7},{5,6},{6,5},{7,4},{8,11},{9,10},{10,... | collective-permute-start | bytes 786440 | tf_op jit(solution)/shard_map/ppermute | solution.py:49
  235.4 12.7 %collective-permute-start.9 = (bf16[512,256]{1,0:T(8,128)(2,1)S(1)}, bf16[512,256]{1,0:T(8,128)(2,1)S(1)}, u32[]{:S(2)}, u32[]{:S(2)}) collective-permute-start(bf16[512,256]{1,0:T(8,128)(2,1)S(1)} %get-tuple-element.57.d0), channel_id=1, source_target_pairs={{0,2},{1,3},{2,0},{3,1},{4,6},{5,7},{6,4},{7,5},{8,10},{9,11},{10,... | collective-permute-start | bytes 786440 | tf_op jit(solution)/shard_map/ppermute | solution.py:49
  235.9 12.2 %collective-permute-start.8 = (bf16[512,256]{1,0:T(8,128)(2,1)S(1)}, bf16[512,256]{1,0:T(8,128)(2,1)S(1)}, u32[]{:S(2)}, u32[]{:S(2)}) collective-permute-start(bf16[512,256]{1,0:T(8,128)(2,1)S(1)} %get-tuple-element.57.d0), channel_id=1, source_target_pairs={{0,1},{1,0},{2,3},{3,2},{4,5},{5,4},{6,7},{7,6},{8,9},{9,8},{10,11... | collective-permute-start | bytes 786440 | tf_op jit(solution)/shard_map/ppermute | solution.py:49
  241.8 6.3 %copy-start.19 = (bf16[512,256]{1,0:T(8,128)(2,1)}, bf16[512,256]{1,0:T(8,128)(2,1)S(1)}, u32[]{:S(2)}) copy-start(bf16[512,256]{1,0:T(8,128)(2,1)S(1)} %collective-permute-done.10.d3) | copy-start | bytes 786436
  248.9 58.0 %all-to-all-start.3 = ((bf16[8,4,32,1024]{3,2,1,0:T(8,128)(2,1)}), bf16[8,4,32,1024]{3,2,1,0:T(8,128)(2,1)}, u32[]{:S(2)}, u32[]{:S(2)}) async-start(bf16[8,4,32,1024]{3,2,1,0:T(8,128)(2,1)} %add_convert_fusion), calls=%async_computation.3 | async-start | bytes 4194304 | tf_op jit(solution)/shard_map/all_to_all | solution.py:61
  260.1 3.8 copy-start.5
  260.4 25.3 %collective-permute-start.13 = (bf16[2,128,1024]{2,1,0:T(8,128)(2,1)S(1)}, bf16[2,128,1024]{2,1,0:T(8,128)(2,1)S(1)}, u32[]{:S(2)}, u32[]{:S(2)}) collective-permute-start(bf16[2,128,1024]{2,1,0:T(8,128)(2,1)S(1)} %get-tuple-element.78), channel_id=1, source_target_pairs={{0,3},{1,2},{2,1},{3,0},{4,7},{5,6},{6,5},{7,4},{8,11},{9,10},{10,... | collective-permute-start | bytes 1572872 | tf_op jit(solution)/shard_map/ppermute | solution.py:49
  262.0 34.9 %collective-permute-start.12 = (bf16[2,128,1024]{2,1,0:T(8,128)(2,1)S(1)}, bf16[2,128,1024]{2,1,0:T(8,128)(2,1)S(1)}, u32[]{:S(2)}, u32[]{:S(2)}) collective-permute-start(bf16[2,128,1024]{2,1,0:T(8,128)(2,1)S(1)} %get-tuple-element.79), channel_id=1, source_target_pairs={{0,2},{1,3},{2,0},{3,1},{4,6},{5,7},{6,4},{7,5},{8,10},{9,11},{10,... | collective-permute-start | bytes 1572872 | tf_op jit(solution)/shard_map/ppermute | solution.py:49
  262.8 43.4 %collective-permute-start.11 = (bf16[2,128,1024]{2,1,0:T(8,128)(2,1)S(1)}, bf16[2,128,1024]{2,1,0:T(8,128)(2,1)S(1)}, u32[]{:S(2)}, u32[]{:S(2)}) collective-permute-start(bf16[2,128,1024]{2,1,0:T(8,128)(2,1)S(1)} %get-tuple-element.80), channel_id=1, source_target_pairs={{0,1},{1,0},{2,3},{3,2},{4,5},{5,4},{6,7},{7,6},{8,9},{9,8},{10,11... | collective-permute-start | bytes 1572872 | tf_op jit(solution)/shard_map/ppermute | solution.py:49
  326.2 44.2 %all-to-all-start.5 = ((f32[8,32,1024]{2,1,0:T(8,128)}), f32[8,32,1024]{2,1,0:T(8,128)}, u32[]{:S(2)}, u32[]{:S(2)}) async-start(f32[8,32,1024]{2,1,0:T(8,128)} %broadcast_in_dim.12), calls=%async_computation.5 | async-start | bytes 2097152 | tf_op jit(solution)/shard_map/all_to_all | solution.py:61
  336.2 22.1 %collective-permute-start.16 = (bf16[128,2048]{1,0:T(8,128)(2,1)S(1)}, bf16[128,2048]{1,0:T(8,128)(2,1)S(1)}, u32[]{:S(2)}, u32[]{:S(2)}) collective-permute-start(bf16[128,2048]{1,0:T(8,128)(2,1)S(1)} %get-tuple-element.74), channel_id=1, source_target_pairs={{0,3},{1,2},{2,1},{3,0},{4,7},{5,6},{6,5},{7,4},{8,11},{9,10},{10,... | collective-permute-start | bytes 1572872 | tf_op jit(solution)/shard_map/ppermute | solution.py:49
  340.3 29.3 %collective-permute-start.15 = (bf16[128,2048]{1,0:T(8,128)(2,1)S(1)}, bf16[128,2048]{1,0:T(8,128)(2,1)S(1)}, u32[]{:S(2)}, u32[]{:S(2)}) collective-permute-start(bf16[128,2048]{1,0:T(8,128)(2,1)S(1)} %get-tuple-element.75), channel_id=1, source_target_pairs={{0,2},{1,3},{2,0},{3,1},{4,6},{5,7},{6,4},{7,5},{8,10},{9,11},{10,... | collective-permute-start | bytes 1572872 | tf_op jit(solution)/shard_map/ppermute | solution.py:49
  340.3 30.1 %collective-permute-start.14 = (bf16[128,2048]{1,0:T(8,128)(2,1)S(1)}, bf16[128,2048]{1,0:T(8,128)(2,1)S(1)}, u32[]{:S(2)}, u32[]{:S(2)}) collective-permute-start(bf16[128,2048]{1,0:T(8,128)(2,1)S(1)} %get-tuple-element.76), channel_id=1, source_target_pairs={{0,1},{1,0},{2,3},{3,2},{4,5},{5,4},{6,7},{7,6},{8,9},{9,8},{10,11... | collective-permute-start | bytes 1572872 | tf_op jit(solution)/shard_map/ppermute | solution.py:49
  370.3 9.1 %collective-permute-start.17 = (f32[256,1024]{1,0:T(8,128)}, f32[256,1024]{1,0:T(8,128)}, u32[]{:S(2)}, u32[]{:S(2)}) collective-permute-start(f32[256,1024]{1,0:T(8,128)} %bitcast.12), channel_id=1, source_target_pairs={{0,16},{16,0},{1,17},{17,1},{2,18},{18,2},{3,19},{19,3},{4,20},{20... | collective-permute-start | bytes 3145736 | tf_op jit(solution)/shard_map/ppermute | solution.py:49
  (15 other events, 14.4 us)
Sparse Core Ops, SparseCore 0:
  10.5 71.7 all-gather.1
